TPU v7x, 32 devices: a whole 2x2x4 slice. The times are simulated.
32 devices in a mesh: rep: 8 (over z, core), zero: 4 (over y, x).
Axes of the slice: x: 2, y: 2, z: 4, core: 2. Of those that a mesh axis runs over, the one named last changes fastest.
Arguments:
- tokens: bfloat16 [32768, 1024], P(('rep', 'zero')), may hold values from -6 to 6
- segment_ids: int32 [32768], P(('rep', 'zero')), may hold values from 0 to 63, never falling along the last dimension, each value on 1 to 2048 neighbouring positions
- cotangent: bfloat16 [32768, 1024], P(('rep', 'zero')), may hold values from -6 to 6
- lead_gain: float32 [1024], P('zero'), may hold values from 0.25 to 1.75
- inner_weight: float32 [1024, 4384], P('zero'), may hold values from -0.1875 to 0.1875
- conv_table: float32 [5, 2304], P(None, 'zero'), may hold values from -3 to 3
- head_table: float32 [3, 32], P(None, 'zero'), may hold values from -6 to 2, as said below
- gate_gain: float32 [2048], P('zero'), may hold values from 0.25 to 1.75
- outer_weight: float32 [2048, 1024], P('zero'), may hold values from -0.125 to 0.125
- lead_first: float32 [1024], P('zero'), may hold values from -6 to 6
- inner_first: float32 [1024, 4384], P('zero'), may hold values from -6 to 6
- conv_first: float32 [5, 2304], P(None, 'zero'), may hold values from -6 to 6
- head_first: float32 [3, 32], P(None, 'zero'), may hold values from -6 to 6
- gate_first: float32 [2048], P('zero'), may hold values from -6 to 6
- outer_first: float32 [2048, 1024], P('zero'), may hold values from -6 to 6
- lead_second: float32 [1024], P('zero'), may hold values from 1 to 100
- inner_second: float32 [1024, 4384], P('zero'), may hold values from 1 to 100
- conv_second: float32 [5, 2304], P(None, 'zero'), may hold values from 1 to 100
- head_second: float32 [3, 32], P(None, 'zero'), may hold values from 1 to 100
- gate_second: float32 [2048], P('zero'), may hold values from 1 to 100
- outer_second: float32 [2048, 1024], P('zero'), may hold values from 1 to 100
Outputs:
- mixed: bfloat16 [32768, 1024], P(('rep', 'zero'))
- tokens_grad: bfloat16 [32768, 1024], P(('rep', 'zero'))
- lead_grad: float32 [1024], P('zero')
- inner_grad: float32 [1024, 4384], P('zero')
- conv_grad: float32 [5, 2304], P(None, 'zero')
- head_grad: float32 [3, 32], P(None, 'zero')
- gate_grad: float32 [2048], P('zero')
- outer_grad: float32 [2048, 1024], P('zero')
- lead_fresh: float32 [1024], P('zero')
- inner_fresh: float32 [1024, 4384], P('zero')
- conv_fresh: float32 [5, 2304], P(None, 'zero')
- head_fresh: float32 [3, 32], P(None, 'zero')
- gate_fresh: float32 [2048], P('zero')
- outer_fresh: float32 [2048, 1024], P('zero')
- first_lead: float32 [1024], P('zero')
- first_inner: float32 [1024, 4384], P('zero')
- first_conv: float32 [5, 2304], P(None, 'zero')
- first_head: float32 [3, 32], P(None, 'zero')
- first_gate: float32 [2048], P('zero')
- first_outer: float32 [2048, 1024], P('zero')
- second_lead: float32 [1024], P('zero')
- second_inner: float32 [1024, 4384], P('zero')
- second_conv: float32 [5, 2304], P(None, 'zero')
- second_head: float32 [3, 32], P(None, 'zero')
- second_gate: float32 [2048], P('zero')
- second_outer: float32 [2048, 1024], P('zero')
Inputs may be any that keep to these rules, and one draw needn't show every extreme that they name: `segment_ids`: document numbers never fall along the tokens; a sequence begins a new scan and convolution at its first token even if its document continued in the previous sequence. `head_table`: row 0 lies in -6 to -2, row 1 in 0 to 2, row 2 in 1 to 2.
All inputs are finite; a program needn't handle non-finite values.
Results may differ from a plain program's by a relative error of at most 0.025.
Values may be sent and summed in bfloat16 or wider, within the bound.
No kernel may reach another device: no remote copies, remote signals or barrier semaphores. Data moves between devices by JAX's collectives and lax.ppermute only.
A program may use at most 256 MiB of HBM per device.

v0:
```python
import jax
import jax.numpy as jnp
from jax import lax
from jax.sharding import PartitionSpec as P

DI = 2048
H = 32
P_SIZE = 64
N = 128
K = 4
BLOCK = 256
LEN = 1024
CONV = 2304


norm_eps = 1e-05
beta_one = 0.9
beta_two = 0.95
learn_rate = 0.01
decay_rate = 0.1
adam_eps = 1e-08
adam_step = 3
highest = lax.Precision.HIGHEST


def lead_norm(inputs, gain):
    return inputs * lax.rsqrt(jnp.mean(inputs * inputs, axis=-1, keepdims=True) + norm_eps) * gain


def convolve(conv_in, kernel, doc_ids):
    summed = kernel[K] + conv_in * kernel[K - 1]
    for step_back in range(1, K):
        shifted = jnp.concatenate(
            [jnp.zeros((step_back, conv_in.shape[1]), jnp.float32), conv_in[:-step_back]], axis=0
        )
        before = jnp.concatenate([jnp.full((step_back,), -1, jnp.int32), doc_ids[:-step_back]])
        summed = (
            summed
            + jnp.where((before == doc_ids)[:, None], shifted, 0.0) * kernel[K - 1 - step_back]
        )
    return summed


def mix_blocks(values, entry_b, entry_c, steps, rates, doc_ids):
    memory = jnp.zeros((H, P_SIZE, N), jnp.float32)
    previous = jnp.int32(-1)
    causal = lax.broadcasted_iota(jnp.int32, (BLOCK, BLOCK), 0) >= lax.broadcasted_iota(
        jnp.int32, (BLOCK, BLOCK), 1
    )
    pieces = []
    for number in range(values.shape[0] // BLOCK):
        offset = number * BLOCK
        block_x = values[offset : offset + BLOCK]
        block_b = entry_b[offset : offset + BLOCK]
        block_c = entry_c[offset : offset + BLOCK]
        block_dt = steps[offset : offset + BLOCK]
        block_ids = doc_ids[offset : offset + BLOCK]
        log_decay = jnp.cumsum(block_dt * rates, axis=0)
        linked = causal & (block_ids[:, None] == block_ids[None, :])
        spread = log_decay.T[:, :, None] - log_decay.T[:, None, :]
        decays = jnp.where(linked, jnp.exp(jnp.where(linked, spread, 0.0)), 0.0)
        scores = jnp.dot(
            block_c.astype(jnp.bfloat16),
            block_b.astype(jnp.bfloat16).T,
            preferred_element_type=jnp.float32,
        )
        weights = decays * scores * block_dt.T[:, None, :]
        result = jnp.einsum("hts,shp->thp", weights, block_x, precision=highest)
        carried = jnp.where((block_ids == previous)[:, None], jnp.exp(log_decay), 0.0)
        result = (
            result
            + jnp.einsum("tn,hpn->thp", block_c, memory, precision=highest) * carried[:, :, None]
        )
        last_id = block_ids[BLOCK - 1]
        ending = (
            jnp.where(
                (block_ids == last_id)[:, None],
                jnp.exp(log_decay[BLOCK - 1][None, :] - log_decay),
                0.0,
            )
            * block_dt
        )
        carry_keep = jnp.where(last_id == previous, jnp.exp(log_decay[BLOCK - 1]), 0.0)
        memory = memory * carry_keep[:, None, None] + jnp.einsum(
            "sh,shp,sn->hpn", ending, block_x, block_b, precision=highest
        )
        previous = last_id
        pieces.append(result)
    return jnp.concatenate(pieces, axis=0)


def mix_sequence(gate_in, step_in, acts, heads, gain, doc_ids):
    steps = jax.nn.softplus(step_in + heads[0])
    rates = -jnp.exp(heads[1])
    values = acts[:, :DI].reshape(-1, H, P_SIZE)
    mixed_y = mix_blocks(values, acts[:, DI : DI + N], acts[:, DI + N :], steps, rates, doc_ids)
    mixed_y = mixed_y + heads[2][None, :, None] * values
    gated = mixed_y.reshape(-1, DI) * jax.nn.silu(gate_in)
    return gated * lax.rsqrt(jnp.mean(gated * gated, axis=-1, keepdims=True) + norm_eps) * gain


def adam(weight, grad, first, second):
    first_new = beta_one * first + (1.0 - beta_one) * grad
    second_new = beta_two * second + (1.0 - beta_two) * grad * grad
    first_hat = first_new / (1.0 - beta_one**adam_step)
    second_hat = second_new / (1.0 - beta_two**adam_step)
    fresh = weight - learn_rate * (
        first_hat / (jnp.sqrt(second_hat) + adam_eps) + decay_rate * weight
    )
    return (fresh, first_new, second_new)


def body(
    tokens,
    segment_ids,
    cotangent,
    lead_gain,
    inner_weight,
    conv_table,
    head_table,
    gate_gain,
    outer_weight,
    lead_first,
    inner_first,
    conv_first,
    head_first,
    gate_first,
    outer_first,
    lead_second,
    inner_second,
    conv_second,
    head_second,
    gate_second,
    outer_second,
):
    gathered = (
        lax.all_gather(lead_gain.astype(jnp.bfloat16), "zero", axis=0, tiled=True),
        lax.all_gather(inner_weight.astype(jnp.bfloat16), "zero", axis=0, tiled=True),
        lax.all_gather(conv_table.astype(jnp.bfloat16), "zero", axis=1, tiled=True),
        lax.all_gather(head_table.astype(jnp.bfloat16), "zero", axis=1, tiled=True),
        lax.all_gather(gate_gain.astype(jnp.bfloat16), "zero", axis=0, tiled=True),
        lax.all_gather(outer_weight.astype(jnp.bfloat16), "zero", axis=0, tiled=True),
    )
    lead_low, inner_low, conv_low, head_low, gate_low, outer_low = gathered
    row_count = tokens.shape[0]
    sequences = row_count // LEN
    doc_ids = segment_ids.reshape(sequences, LEN)
    inputs = tokens.astype(jnp.float32)
    normed, lead_pull = jax.vjp(lead_norm, inputs, lead_low.astype(jnp.float32))
    normed_low = normed.astype(jnp.bfloat16)
    projected = jnp.dot(normed_low, inner_low, preferred_element_type=jnp.float32)
    gate_in = projected[:, :DI].reshape(sequences, LEN, DI)
    conv_in = projected[:, DI : DI + CONV].reshape(sequences, LEN, CONV)
    step_in = projected[:, DI + CONV :].reshape(sequences, LEN, H)

    def conv_section(signal, kernel):
        return jax.nn.silu(jax.vmap(convolve, in_axes=(0, None, 0))(signal, kernel, doc_ids))

    activated, conv_pull = jax.vjp(conv_section, conv_in, conv_low.astype(jnp.float32))
    acts = lax.optimization_barrier(activated.astype(jnp.bfloat16)).astype(jnp.float32)

    def mix_section(gate_part, step_part, signal, heads, gain):
        return jax.vmap(mix_sequence, in_axes=(0, 0, 0, None, None, 0))(
            gate_part, step_part, signal, heads, gain, doc_ids
        )

    gnormed, mix_pull = jax.vjp(
        mix_section,
        gate_in,
        step_in,
        acts,
        head_low.astype(jnp.float32),
        gate_low.astype(jnp.float32),
    )
    gnormed_low = gnormed.reshape(row_count, DI).astype(jnp.bfloat16)
    mixed = (inputs + jnp.dot(gnormed_low, outer_low, preferred_element_type=jnp.float32)).astype(
        jnp.bfloat16
    )
    outer_grad = jnp.einsum("td,te->de", gnormed_low, cotangent, preferred_element_type=jnp.float32)
    gn_grad = jnp.einsum("te,de->td", cotangent, outer_low, preferred_element_type=jnp.float32)
    gate_in_grad, step_in_grad, acts_grad, head_grad, gate_grad = mix_pull(
        gn_grad.reshape(sequences, LEN, DI)
    )
    conv_in_grad, conv_grad = conv_pull(acts_grad)
    proj_grad = jnp.concatenate(
        [
            gate_in_grad.reshape(row_count, DI),
            conv_in_grad.reshape(row_count, CONV),
            step_in_grad.reshape(row_count, H),
        ],
        axis=1,
    ).astype(jnp.bfloat16)
    inner_grad = jnp.einsum("td,tp->dp", normed_low, proj_grad, preferred_element_type=jnp.float32)
    normed_grad = jnp.einsum("tp,dp->td", proj_grad, inner_low, preferred_element_type=jnp.float32)
    input_grad, lead_grad = lead_pull(normed_grad)
    tokens_grad = (cotangent.astype(jnp.float32) + input_grad).astype(jnp.bfloat16)
    partial_sums = (
        lax.psum_scatter(
            lead_grad.astype(jnp.bfloat16), "zero", scatter_dimension=0, tiled=True
        ).astype(jnp.float32),
        lax.psum_scatter(
            inner_grad.astype(jnp.bfloat16), "zero", scatter_dimension=0, tiled=True
        ).astype(jnp.float32),
        lax.psum_scatter(
            conv_grad.astype(jnp.bfloat16), "zero", scatter_dimension=1, tiled=True
        ).astype(jnp.float32),
        lax.psum_scatter(
            head_grad.astype(jnp.bfloat16), "zero", scatter_dimension=1, tiled=True
        ).astype(jnp.float32),
        lax.psum_scatter(
            gate_grad.astype(jnp.bfloat16), "zero", scatter_dimension=0, tiled=True
        ).astype(jnp.float32),
        lax.psum_scatter(
            outer_grad.astype(jnp.bfloat16), "zero", scatter_dimension=0, tiled=True
        ).astype(jnp.float32),
    )
    owner_sums = (
        lax.psum(partial_sums[0].astype(jnp.bfloat16), "rep").astype(jnp.float32),
        lax.psum(partial_sums[1].astype(jnp.bfloat16), "rep").astype(jnp.float32),
        lax.psum(partial_sums[2].astype(jnp.bfloat16), "rep").astype(jnp.float32),
        lax.psum(partial_sums[3].astype(jnp.bfloat16), "rep").astype(jnp.float32),
        lax.psum(partial_sums[4].astype(jnp.bfloat16), "rep").astype(jnp.float32),
        lax.psum(partial_sums[5].astype(jnp.bfloat16), "rep").astype(jnp.float32),
    )
    lead_up = adam(lead_gain, owner_sums[0], lead_first, lead_second)
    inner_up = adam(inner_weight, owner_sums[1], inner_first, inner_second)
    conv_up = adam(conv_table, owner_sums[2], conv_first, conv_second)
    head_up = adam(head_table, owner_sums[3], head_first, head_second)
    gate_up = adam(gate_gain, owner_sums[4], gate_first, gate_second)
    outer_up = adam(outer_weight, owner_sums[5], outer_first, outer_second)
    return (
        mixed,
        tokens_grad,
        owner_sums[0],
        owner_sums[1],
        owner_sums[2],
        owner_sums[3],
        owner_sums[4],
        owner_sums[5],
        lead_up[0],
        inner_up[0],
        conv_up[0],
        head_up[0],
        gate_up[0],
        outer_up[0],
        lead_up[1],
        inner_up[1],
        conv_up[1],
        head_up[1],
        gate_up[1],
        outer_up[1],
        lead_up[2],
        inner_up[2],
        conv_up[2],
        head_up[2],
        gate_up[2],
        outer_up[2],
    )


def solution(mesh):
    return jax.shard_map(
        body,
        mesh=mesh,
        in_specs=(
            P(("rep", "zero"), None),
            P(("rep", "zero")),
            P(("rep", "zero"), None),
            P("zero"),
            P("zero", None),
            P(None, "zero"),
            P(None, "zero"),
            P("zero"),
            P("zero", None),
            P("zero"),
            P("zero", None),
            P(None, "zero"),
            P(None, "zero"),
            P("zero"),
            P("zero", None),
            P("zero"),
            P("zero", None),
            P(None, "zero"),
            P(None, "zero"),
            P("zero"),
            P("zero", None),
        ),
        out_specs=(
            P(("rep", "zero"), None),
            P(("rep", "zero"), None),
            P("zero"),
            P("zero", None),
            P(None, "zero"),
            P(None, "zero"),
            P("zero"),
            P("zero", None),
            P("zero"),
            P("zero", None),
            P(None, "zero"),
            P(None, "zero"),
            P("zero"),
            P("zero", None),
            P("zero"),
            P("zero", None),
            P(None, "zero"),
            P(None, "zero"),
            P("zero"),
            P("zero", None),
            P("zero"),
            P("zero", None),
            P(None, "zero"),
            P(None, "zero"),
            P("zero"),
            P("zero", None),
        ),
        check_vma=False,
    )
```

profile of v0, /device:TPU:0, one launch (start us, length us, event | category | flops | bytes accessed | tf_op | source)
XLA Modules:
  0.0 810.5 jit_solution(11497283500332110642)
XLA Ops:
  61.2 45.5 %all-gather.7.cloned.1.call-done = bf16[1024,4384]{0,1:T(8,128)(2,1)} async-done(((bf16[256,4384]{0,1:T(8,128)(2,1)}), bf16[1024,4384]{0,1:T(8,128)(2,1)}) %all-gather.7.cloned.1.call-update) | async-done | bytes 8978448 | tf_op jit(solution)/shard_map/all_gather | solution.py:138
  106.7 13.1 %fusion.278 = f32[1024,4384]{0,1:T(8,128)S(1)} fusion(bf16[1024,4384]{0,1:T(8,128)(2,1)} %all-gather.7.cloned.1.call-done, bf16[1024,1024]{1,0:T(8,128)(2,1)} %param.21, f32[1024]{0:T(1024)S(1)} %bitcast.1021, f32[1024]{0:T(1024)S(1)} %fusion.379), kind=kOutput, calls=%fused_computation.312 | convolution fusion | flops 9198108672 | bytes 29040640 | tf_op jit(solution)/shard_map/dot_general | solution.py:151
  137.6 15.2 %multiply_convert_fusion = (bf16[1,1024,2304]{1,2,0:T(8,128)(2,1)S(1)}, f32[1,1024,2304]{1,2,0:T(8,128)}) fusion(f32[2304]{0:T(1024)S(1)} %get-tuple-element.65, f32[1,1021,2304]{1,2,0:T(8,128)S(1)} %bitcast.926, pred[1024]{0:T(1024)(128)(4,1)S(1)} %get-tuple-element.77, f32[2304]{0:T(1024)S(1)} %get-tuple-element.66, f32[1,1022,2304]{1,2,0:T(8,128)S(1)} %bitcast.927, ...), kind=kLoop, calls=%fused_computation.22 | loop fusion | flops 37748736 | bytes 51898368 | tf_op jit(solution)/shard_map/convert_element_type | solution.py:160
  228.3 14.7 %multiply_reduce_fusion.4 = (bf16[2048]{0:T(1024)(128)(2,1)}, f32[1024]{0:T(1024)S(1)}, f32[1024,2048]{0,1:T(8,128)}) fusion(f32[1024,2048]{0,1:T(8,128)} %copy-done.4, f32[1024]{0:T(1024)} %copy-done.118, f32[2048]{0:T(1024)S(1)} %bitcast.1017, bf16[1024,1024]{1,0:T(8,128)(2,1)} %param.23, bf16[2048,1024]{1,0:T(8,128)(2,1)} %all-gather.9.cloned.1.call-done), kind=kOutput, calls=%fused_computation.35 | convolution fusion | flops 4307547136 | bytes 23089152 | tf_op jit(solution)/shard_map/te,de->td/dot_general | solution.py:180
  243.6 10.1 %fusion.9 = (f32[2048]{0:T(1024)}, f32[1024,2048]{0,1:T(8,128)S(1)}) fusion(bf16[1,1024,2304]{1,2,0:T(8,128)(2,1)} %copy-done.3, f32[1024,4384]{0,1:T(8,128)} %copy-done.2, f32[1024,2048]{0,1:T(8,128)S(1)} %copy-done.5, f32[1024]{0:T(1024)} %multiply_multiply_fusion.4, f32[1024]{0:T(1024)} %copy-done.118, f32[1024,2048]{0,1:T(8,128)} %get-tuple-element.150, ...), kind=kLoop, calls=%fused_computation.31 | loop fusion | flops 27260928 | bytes 37773312 | tf_op jit(solution)/shard_map/transpose(jvp(vmap()))/reduce_sum | solution.py:97
  262.9 11.1 %fusion.49 = (f32[32,256]{1,0:T(8,128)}, f32[32,256]{1,0:T(8,128)}, f32[32,256]{1,0:T(8,128)}, bf16[256,256]{1,0:T(8,128)(2,1)S(1)}) fusion(f32[32,256]{1,0:T(8,128)S(1)} %copy-done.122, f32[256,256]{1,0:T(8,128)S(1)} %copy-done.70, f32[32,256]{1,0:T(8,128)S(1)} %copy-done.125, pred[256,256]{1,0:T(8,128)(4,1)S(1)} %copy-done.106, ...), kind=kOutput, calls=%fused_computation.94 | convolution fusion | flops 1641979904 | bytes 3801088 | tf_op jit(solution)/shard_map/transpose(jvp(vmap(hts,shp->thp)))/dot_general | solution.py:68
  280.9 10.9 %fusion.51 = (f32[32,256]{1,0:T(8,128)}, f32[32,256]{1,0:T(8,128)}, f32[32,256]{1,0:T(8,128)}, bf16[256,256]{1,0:T(8,128)(2,1)S(1)}) fusion(f32[32,256]{1,0:T(8,128)S(1)} %copy-done.132, f32[256,256]{1,0:T(8,128)S(1)} %copy-done.75, f32[32,256]{1,0:T(8,128)S(1)} %copy-done.137, pred[256,256]{1,0:T(8,128)(4,1)S(1)} %copy-done.111, ...), kind=kOutput, calls=%fused_computation.96 | convolution fusion | flops 1641979904 | bytes 3801088 | tf_op jit(solution)/shard_map/transpose(jvp(vmap(hts,shp->thp)))/dot_general | solution.py:68
  295.2 10.9 %fusion.53 = (f32[32,256]{1,0:T(8,128)}, f32[32,256]{1,0:T(8,128)}, f32[32,256]{1,0:T(8,128)}, bf16[256,256]{1,0:T(8,128)(2,1)S(1)}) fusion(f32[32,256]{1,0:T(8,128)S(1)} %copy-done.135, f32[256,256]{1,0:T(8,128)S(1)} %copy-done.78, f32[32,256]{1,0:T(8,128)S(1)} %copy-done.140, pred[256,256]{1,0:T(8,128)(4,1)S(1)} %copy-done.114, ...), kind=kOutput, calls=%fused_computation.98 | convolution fusion | flops 1641979904 | bytes 3801088 | tf_op jit(solution)/shard_map/transpose(jvp(vmap(hts,shp->thp)))/dot_general | solution.py:68
  309.5 10.8 %fusion.47 = (f32[32,256]{1,0:T(8,128)S(1)}, f32[32,256]{1,0:T(8,128)S(1)}, f32[32,256]{1,0:T(8,128)}, bf16[256,256]{1,0:T(8,128)(2,1)S(1)}) fusion(f32[32,256]{1,0:T(8,128)S(1)} %copy-done.128, f32[256,256]{1,0:T(8,128)S(1)} %copy-done.73, f32[32,256]{1,0:T(8,128)S(1)} %copy-done.130, pred[256,256]{1,0:T(8,128)(4,1)S(1)} %copy-done.109, ...), kind=kOutput, calls=%fused_computation.92 | convolution fusion | flops 1641979904 | bytes 3801088 | tf_op jit(solution)/shard_map/transpose(jvp(vmap(hts,shp->thp)))/dot_general | solution.py:68
  339.2 10.0 %bitcast_add_fusion.1 = f32[1,256,32,64]{1,3,2,0:T(8,128)} fusion(f32[32,64,256]{2,1,0:T(8,128)S(1)} %fusion.326, f32[32,256]{1,0:T(8,128)} %copy.310, f32[256,256]{1,0:T(8,128)S(1)} %copy-done.79, f32[32,256]{1,0:T(8,128)} %copy-done.139, pred[256,256]{1,0:T(8,128)(4,1)} %fusion.291, f32[1,1024,32,64]{1,3,2,0:T(8,128)} %bitcast.942, ...), kind=kOutput, calls=%fused_computation.174 | convolution fusion | flops 1622147072 | bytes 6750208 | tf_op jit(solution)/shard_map/transpose(jvp(vmap(hts,shp->thp)))/dot_general | solution.py:68
  354.8 10.0 %bitcast_add_fusion.2 = f32[1,256,32,64]{1,3,2,0:T(8,128)} fusion(f32[32,64,256]{2,1,0:T(8,128)S(1)} %fusion.320, f32[32,256]{1,0:T(8,128)S(1)} %copy-done.133, f32[256,256]{1,0:T(8,128)S(1)} %copy-done.76, f32[32,256]{1,0:T(8,128)S(1)} %copy-done.138, pred[256,256]{1,0:T(8,128)(4,1)S(1)} %copy-done.112, f32[1,1024,32,64]{1,3,2,0:T(8,128)} %bitcast.943, ...), kind=kOutput, calls=%fused_computation.175 | convolution fusion | flops 1622147072 | bytes 6750208 | tf_op jit(solution)/shard_map/transpose(jvp(vmap(hts,shp->thp)))/dot_general | solution.py:68
  483.4 27.2 %multiply_reduce_fusion.3 = (f32[2304]{0:T(1024)S(1)}, f32[2304]{0:T(1024)S(1)}, f32[2304]{0:T(1024)S(1)}, f32[2304]{0:T(1024)S(1)}, f32[2304]{0:T(1024)S(1)}, /*index=5*/f32[1,1024,2304]{1,2,0:T(8,128)}) fusion(f32[1,1021,2304]{1,2,0:T(8,128)} %bitcast.929, pred[1024]{0:T(1024)(128)(4,1)S(1)} %copy-done.148, f32[1024,4384]{0,1:T(8,128)} %copy-done.2, ...), kind=kLoop, calls=%fused_computation.20 | loop fusion | flops 54252288 | bytes 66054144 | tf_op jit(solution)/shard_map/transpose(jvp(vmap()))/reduce_sum | solution.py:39
  510.8 10.3 %fusion.2 = f32[1,1023,2304]{1,2,0:T(8,128)} fusion(f32[1,1024,2304]{1,2,0:T(8,128)} %get-tuple-element.111, f32[2304]{0:T(1024)S(1)} %copy-done.98, pred[1023]{0:T(1024)(128)(4,1)S(1)} %copy-done.184), kind=kLoop, calls=%fused_computation.9 | loop fusion | flops 4713984 | bytes 18866176 | tf_op jit(solution)/shard_map/transpose(jvp(vmap(jit(_where))))/select_n | solution.py:39
  522.1 10.3 %fusion.3 = f32[1,1022,2304]{1,2,0:T(8,128)} fusion(f32[1,1024,2304]{1,2,0:T(8,128)} %get-tuple-element.111, f32[2304]{0:T(1024)S(1)} %copy-done.96, pred[1022]{0:T(1024)(128)(4,1)S(1)} %copy-done.183), kind=kLoop, calls=%fused_computation.11 | loop fusion | flops 4709376 | bytes 18847742 | tf_op jit(solution)/shard_map/transpose(jvp(vmap(jit(_where))))/select_n | solution.py:39
  538.8 12.6 %fusion.44 = bf16[1024,2304]{0,1:T(8,128)(2,1)} fusion(f32[1,1024,2304]{1,2,0:T(8,128)S(1)} %bitcast.933, f32[1,1023,2304]{1,2,0:T(8,128)} %fusion.2, f32[1,1022,2304]{1,2,0:T(8,128)} %fusion.3, f32[1,1021,2304]{1,2,0:T(8,128)} %fusion.4, f32[2304]{0:T(1024)S(1)} %copy-done.92), kind=kLoop, calls=%fused_computation.87 | loop fusion | flops 11796480 | bytes 42421248 | tf_op jit(solution)/shard_map/reshape | solution.py:188
  552.7 12.9 %fusion.12 = bf16[1024,2048]{0,1:T(8,128)(2,1)} fusion(f32[1024,4384]{0,1:T(8,128)} %copy-done.2, f32[1024,2048]{0,1:T(8,128)} %copy-done.4, f32[1024]{0:T(1024)S(1)} %copy-done.117, f32[1024,2048]{0,1:T(8,128)} %get-tuple-element.150, f32[2048]{0:T(1024)S(1)} %bitcast.1019, f32[1024]{0:T(1024)S(1)} %copy-done.119, f32[2048]{0:T(1024)S(1)} %copy-done.102, ...), kind=kLoop, calls=%fused_computation.34 | loop fusion | flops 46137344 | bytes 41967616 | tf_op jit(solution)/shard_map/convert.9
  565.6 18.2 %convolution_convert_fusion = bf16[1024,4384]{0,1:T(8,128)(2,1)} fusion(bf16[1024,32]{0,1:T(8,128)(2,1)S(1)} %copy.376, bf16[1024,2304]{0,1:T(8,128)(2,1)} %fusion.44, bf16[1024,2048]{0,1:T(8,128)(2,1)} %fusion.12, bf16[1024,1024]{1,0:T(8,128)(2,1)S(1)} %copy-done.18, f32[1024]{0:T(1024)S(1)} %bitcast.1022, f32[1024]{0:T(1024)S(1)} %copy-done.154), kind=kOutput, calls=%fused_computation.5 | convolution fusion | flops 9229533184 | bytes 20062208 | tf_op jit(solution)/shard_map/td,tp->dp/dot_general | solution.py:193
  589.2 17.2 %fusion.55 = (bf16[1024]{0:T(1024)(128)(2,1)S(1)}, f32[1024]{0:T(1024)S(1)}, f32[1024,1024]{1,0:T(8,128)}) fusion(bf16[1024,1024]{1,0:T(8,128)(2,1)S(1)} %copy-done.18, f32[1024]{0:T(1024)S(1)} %copy-done.154, f32[1024]{0:T(1024)S(1)} %bitcast.1023, bf16[1024,4384]{0,1:T(8,128)(2,1)} %all-gather.7.cloned.1.call-done, bf16[1024,32]{0,1:T(8,128)(2,1)S(1)} %copy.376, ...), kind=kOutput, calls=%fused_computation.100 | convolution fusion | flops 9228187648 | bytes 24262656 | tf_op jit(solution)/shard_map/tp,dp->td/dot_general | solution.py:194
  615.7 11.0 %fusion.59 = bf16[1024,1024]{1,0:T(8,128)(2,1)} fusion(bf16[1024,1024]{1,0:T(8,128)(2,1)S(1)} %copy-done.18, bf16[2048,1024]{1,0:T(8,128)(2,1)} %all-gather.9.cloned.1.call-done, f32[1024,2048]{0,1:T(8,128)} %copy-done.4, f32[2048]{0:T(1024)S(1)} %bitcast.1020, f32[1024]{0:T(1024)S(1)} %copy-done.119), kind=kOutput, calls=%fused_computation.104 | convolution fusion | flops 4304404480 | bytes 16789504 | tf_op jit(solution)/shard_map/dot_general | solution.py:176
  627.1 47.7 %reduce-scatter.7.cloned.1.call-done = bf16[256,4384]{0,1:T(8,128)(2,1)} async-done(((bf16[1024,4384]{0,1:T(8,128)(2,1)}), bf16[256,4384]{0,1:T(8,128)(2,1)}) %reduce-scatter.7.cloned.1.call-update) | async-done | bytes 2244624 | tf_op jit(solution)/shard_map/reduce_scatter | solution.py:201
  680.0 23.5 %reduce-scatter.11.cloned.1.call-done = bf16[576,5]{1,0:T(8,128)(2,1)} async-done(((bf16[2304,5]{1,0:T(8,128)(2,1)}), bf16[576,5]{1,0:T(8,128)(2,1)}) %reduce-scatter.11.cloned.1.call-update) | async-done | bytes 5776
  704.6 29.3 %all-reduce.44 = (bf16[256]{0:T(256)(128)(2,1)S(1)}, bf16[5,576]{1,0:T(8,128)(2,1)S(1)}, bf16[3,8]{1,0:T(4,128)(2,1)S(1)}, bf16[512]{0:T(512)(128)(2,1)S(1)}) all-reduce(bf16[256]{0:T(256)(128)(2,1)S(1)} %dynamic-slice.1, bf16[5,576]{1,0:T(8,128)(2,1)S(1)} %copy.425, ...), channel_id=1, replica_groups=mesh['rep'=8,'zero'=4] {'rep'}, use_global_device_ids=true, to_apply=%region_48.49 | all-reduce | flops 3672 | bytes 14688 | tf_op jit(solution)/shard_map/psum | solution.py:218
  736.4 50.1 %all-reduce.49.cloned.1.call-done = (bf16[256,4384]{0,1:T(8,128)(2,1)}, bf16[512,1024]{1,0:T(8,128)(2,1)}) async-done(((bf16[256,4384]{0,1:T(8,128)(2,1)}, bf16[512,1024]{1,0:T(8,128)(2,1)}), (bf16[256,4384]{0,1:T(8,128)(2,1)}, bf16[512,1024]{1,0:T(8,128)(2,1)})) %all-reduce.49.cloned.1.call-update) | async-done | bytes 3293200 | tf_op jit(solution)/shard_map/psum | solution.py:219
  793.2 10.0 %multiply_subtract_fusion = (f32[256,4384]{0,1:T(8,128)}, f32[256,4384]{0,1:T(8,128)}, f32[256,4384]{0,1:T(8,128)}, f32[256,4384]{0,1:T(8,128)}) fusion(f32[256,4384]{0,1:T(8,128)S(1)} %bitcast.971, f32[256,4384]{0,1:T(8,128)} %param.31, f32[256,4384]{0,1:T(8,128)} %param.37, bf16[256,4384]{0,1:T(8,128)(2,1)S(1)} %copy-done.38), kind=kLoop, calls=%fused_computation.89 | loop fusion | flops 17956864 | bytes 33669120 | tf_op jit(solution)/shard_map/sub | solution.py:107
  (665 shorter events, 345.3 us)
Async XLA Ops:
  7.3 99.4 %all-gather.7.cloned.1.call-start = ((), (), s32[]{:S(2)}) async-start(), calls=%async_computation.3 | async-start | bytes 11223040 | tf_op jit(solution)/shard_map/all_gather | solution.py:138
  11.3 216.9 %all-gather.9.cloned.1.call-start = ((), (), s32[]{:S(2)}) async-start(), calls=%async_computation.4 | async-start | bytes 5242880 | tf_op jit(solution)/shard_map/all_gather | solution.py:142
  12.6 614.5 %reduce-scatter.9.cloned.1.call-start = ((), (), s32[]{:S(2)}) async-start(), calls=%async_computation.6 | async-start | bytes 5242880 | tf_op jit(solution)/shard_map/reduce_scatter | solution.py:213
  13.4 124.1 %copy-start.149 = (pred[1024]{0:T(1024)(128)(4,1)}, pred[1024]{0:T(1024)(128)(4,1)S(1)}, u32[]{:S(2)}) copy-start(pred[1024]{0:T(1024)(128)(4,1)S(1)} %add_compare_fusion) | copy-start | bytes 3076
  17.4 120.1 %copy-start.145 = (pred[1024]{0:T(1024)(128)(4,1)}, pred[1024]{0:T(1024)(128)(4,1)S(1)}, u32[]{:S(2)}) copy-start(pred[1024]{0:T(1024)(128)(4,1)S(1)} %get-tuple-element.76) | copy-start | bytes 3076
  17.4 120.1 %copy-start.147 = (pred[1024]{0:T(1024)(128)(4,1)}, pred[1024]{0:T(1024)(128)(4,1)S(1)}, u32[]{:S(2)}) copy-start(pred[1024]{0:T(1024)(128)(4,1)S(1)} %get-tuple-element.77) | copy-start | bytes 3076
  47.7 163.2 %copy-start.101 = (f32[2048]{0:T(1024)}, f32[2048]{0:T(1024)S(1)}, u32[]{:S(2)}) copy-start(f32[2048]{0:T(1024)S(1)} %mul.1038) | copy-start | bytes 24580
  435.6 239.2 %reduce-scatter.7.cloned.1.call-start = ((), (), s32[]{:S(2)}) async-start(), calls=%async_computation.5 | async-start | bytes 11223040 | tf_op jit(solution)/shard_map/reduce_scatter | solution.py:201
  583.8 119.7 %reduce-scatter.11.cloned.1.call-start = ((), (), s32[]{:S(2)}) async-start(), calls=%async_computation.7 | async-start | bytes 737280
  588.4 198.1 %all-reduce.49.cloned.1.call-start = ((), (), s32[]{:S(2)}) async-start(), calls=%async_computation.8 | async-start | bytes 6586368 | tf_op jit(solution)/shard_map/psum | solution.py:219
  626.7 107.1 %copy-start.196 = (f32[256]{0:T(256)S(1)}, f32[256]{0:T(256)}, u32[]{:S(2)}) copy-start(f32[256]{0:T(256)} %param.24) | copy-start | bytes 3076
  626.7 107.1 %copy-start.197 = (f32[256]{0:T(256)S(1)}, f32[256]{0:T(256)}, u32[]{:S(2)}) copy-start(f32[256]{0:T(256)} %param.30) | copy-start | bytes 3076
  626.7 107.1 %copy-start.198 = (f32[256]{0:T(256)S(1)}, f32[256]{0:T(256)}, u32[]{:S(2)}) copy-start(f32[256]{0:T(256)} %param.36) | copy-start | bytes 3076
  626.7 107.7 %copy-start.164 = (f32[3,8]{1,0:T(4,128)S(1)}, f32[3,8]{1,0:T(4,128)}, u32[]{:S(2)}) copy-start(f32[3,8]{1,0:T(4,128)} %param.27) | copy-start | bytes 292
  626.8 107.7 %copy-start.188 = (f32[3,8]{1,0:T(4,128)S(1)}, f32[3,8]{1,0:T(4,128)}, u32[]{:S(2)}) copy-start(f32[3,8]{1,0:T(4,128)} %param.33) | copy-start | bytes 292
  626.8 107.7 %copy-start.189 = (f32[3,8]{1,0:T(4,128)S(1)}, f32[3,8]{1,0:T(4,128)}, u32[]{:S(2)}) copy-start(f32[3,8]{1,0:T(4,128)} %param.39) | copy-start | bytes 292
  626.8 108.3 %copy-start.166 = (f32[512]{0:T(512)S(1)}, f32[512]{0:T(512)}, u32[]{:S(2)}) copy-start(f32[512]{0:T(512)} %param.28) | copy-start | bytes 6148
  626.8 108.3 %copy-start.190 = (f32[512]{0:T(512)S(1)}, f32[512]{0:T(512)}, u32[]{:S(2)}) copy-start(f32[512]{0:T(512)} %param.34) | copy-start | bytes 6148
  626.8 108.3 %copy-start.191 = (f32[512]{0:T(512)S(1)}, f32[512]{0:T(512)}, u32[]{:S(2)}) copy-start(f32[512]{0:T(512)} %param.40) | copy-start | bytes 6148
  626.8 108.9 %copy-start.100 = (f32[5,576]{1,0:T(8,128)S(1)}, f32[5,576]{1,0:T(8,128)}, u32[]{:S(2)}) copy-start(f32[5,576]{1,0:T(8,128)} %param.26) | copy-start | bytes 34564
  626.8 108.9 %copy-start.141 = (f32[5,576]{1,0:T(8,128)S(1)}, f32[5,576]{1,0:T(8,128)}, u32[]{:S(2)}) copy-start(f32[5,576]{1,0:T(8,128)} %param.32) | copy-start | bytes 34564
  626.8 108.9 %copy-start.142 = (f32[5,576]{1,0:T(8,128)S(1)}, f32[5,576]{1,0:T(8,128)}, u32[]{:S(2)}) copy-start(f32[5,576]{1,0:T(8,128)} %param.38) | copy-start | bytes 34564
  626.8 159.6 %copy-start.17 = (f32[512,1024]{1,0:T(8,128)S(1)}, f32[512,1024]{1,0:T(8,128)}, u32[]{:S(2)}) copy-start(f32[512,1024]{1,0:T(8,128)} %param.29) | copy-start | bytes 6291460
  680.0 113.2 %slice-start.7 = ((s8[4489216]{0:T(1024)(128)(4,1)}), s8[294912]{0:T(1024)(128)(4,1)S(1)}, s32[]{:S(2)}) async-start(s8[4489216]{0:T(1024)(128)(4,1)} %bitcast.970), calls=%async_computation.16 | async-start | bytes 589824
  (191 other events, 3690.7 us)
Sparse Core Ops, SparseCore 0:
  11.4 95.2 all-gather.6
  108.6 52.5 all-gather.8
  435.8 51.9 reduce-scatter.8
  584.0 90.8 reduce-scatter.6
  678.1 25.4 reduce-scatter.10
  705.9 80.5 all-reduce.48
where the time goes:
time: 822 us; the launch traced here: 810 us
  matrix products  268 us (33%)
  other arithmetic  202 us (25%)
  waiting for transfers between devices  167 us (20%)
  local copies, waits for them, and re-layouts  78.9 us (10%)
  blocking collectives  72.3 us (9%)
  between operations  22.6 us (3%)
    dot_general x12, matrix products, mix_blocks(): result = jnp.einsum('hts,shp->thp', weights, block_x, precision=highest)  110 us
    psum x1, waiting for transfers between devices, body(): lax.psum(partial_sums[1].astype(jnp.bfloat16), 'rep').astype(jnp.float32)  50.1 us
    reduce_scatter x1, waiting for transfers between devices, body(): lax.psum_scatter(inner_grad.astype(jnp.bfloat16), 'zero', scatter_dimensi...  47.7 us
    all_gather x1, waiting for transfers between devices, body(): lax.all_gather(inner_weight.astype(jnp.bfloat16), 'zero', axis=0, tiled=T...  45.5 us
    another operation x21, other arithmetic  32.4 us
    dot_general x11, matrix products, mix_blocks(): jnp.einsum('tn,hpn->thp', block_c, memory, precision=highest)  32.2 us
    psum x1, blocking collectives, body(): lax.psum(partial_sums[0].astype(jnp.bfloat16), 'rep').astype(jnp.float32)  29.3 us
    dot_general x9, matrix products, mix_blocks(): jnp.einsum('sh,shp,sn->hpn', ending, block_x, block_b, precision=highest)  27.5 us
  transfers between devices with their start and end apart: 6, of which 4 were waited for; matrix products, arithmetic and copies ran while one was open for 38% of the time, Pallas kernels for 0%

commit v1 on v0

v1 whole, which is shorter than its diff:
```python
import jax
import jax.numpy as jnp
from jax import lax
from jax.experimental import pallas as pl
from jax.experimental.pallas import tpu as pltpu
from jax.sharding import PartitionSpec as P

DI = 2048
H = 32
N = 128
K = 4
Q = 128
LEN = 1024
CONV = 2304
WIDE = CONV + H
CH = LEN // Q
PAIRS = H // 2
norm_eps = 1e-05
LOG2E = 1.4426950408889634
NEG = -1e30
f32 = jnp.float32
bf16 = jnp.bfloat16
highest = lax.Precision.HIGHEST


def sigmoid(v):
    return 0.5 * jnp.tanh(0.5 * v) + 0.5


def dot(a, b):
    return jnp.dot(a, b, preferred_element_type=f32)


def dot_nt(a, b):
    return lax.dot_general(a, b, (((1,), (1,)), ((), ())), preferred_element_type=f32)


def lanes(col, width=128):
    return jnp.broadcast_to(col, (col.shape[0], width))


def iota(shape, dim):
    return lax.broadcasted_iota(jnp.int32, shape, dim)


def softplus(v):
    u = jnp.exp(-jnp.abs(v))
    series = u * (1.0 - u * (0.5 - u * (1.0 / 3.0 - u * 0.25)))
    return jnp.maximum(v, 0.0) + jnp.where(u < 0.01, series, jnp.log(1.0 + u))


def decay_terms(step, head):
    pre = step + head[0:1, :]
    dt = softplus(pre)
    lower = (iota((Q, Q), 0) >= iota((Q, Q), 1)).astype(f32)
    a = jnp.dot(lower, dt * head[1:2, :], precision=highest, preferred_element_type=f32) * LOG2E
    b = a - jnp.log(dt) * LOG2E
    return pre, dt, a, b


def fwd_kernel(ids_s, cin, step, rows, taps, head, dskip, y_out, act_out, ds_out, st_out, state, xs, cs, xe, keep):
    c = pl.program_id(0)

    @pl.when(c == 0)
    def _():
        state[...] = jnp.zeros_like(state)
        xs[0:8, :] = jnp.zeros((8, CONV), f32)

    turned = rows[0].T
    m1 = lanes(turned[:, 1:2])
    m2 = lanes(turned[:, 2:3])
    m3 = lanes(turned[:, 3:4])

    def conv_tile(i, _):
        at = pl.ds(pl.multiple_of(i * 128, 128), 128)
        xs[8:136, at] = cin[:, at].astype(f32)
        x0 = xs[8:136, at]
        out = taps[4:5, at] + x0 * taps[3:4, at]
        out += xs[7:135, at] * m1 * taps[2:3, at]
        out += xs[6:134, at] * m2 * taps[1:2, at]
        out += xs[5:133, at] * m3 * taps[0:1, at]
        sig = sigmoid(out)
        act = out * sig
        act_out[:, at] = act.astype(bf16)
        ds_out[:, at] = (sig + act * (1.0 - sig)).astype(bf16)
        return 0

    lax.fori_loop(0, CONV // 128, conv_tile, 0)
    xs[0:8, :] = xs[128:136, :]

    pre, dt, a, b = decay_terms(step[...], head)
    a_t = a.T
    b_t = b.T
    bb = act_out[:, DI : DI + N]
    cc = act_out[:, DI + N :]
    g = dot_nt(cc, bb)
    row_id = lanes(turned[:, 0:1])
    linked = (iota((Q, Q), 0) >= iota((Q, Q), 1)) & (row_id == rows[0, 0:1, :])
    bias = jnp.where(linked, 0.0, NEG)
    prev = jnp.where(c == 0, -1, ids_s[jnp.maximum(c * Q - 1, 0)])
    last = ids_s[c * Q + Q - 1]
    carried = jnp.where(row_id == prev.astype(f32), 0.0, NEG)
    ending = jnp.where(row_id == last.astype(f32), 0.0, NEG)
    kept = jnp.where(last == prev, 0.0, NEG)
    s_low = state[...].astype(bf16)
    st_out[0] = s_low
    cs[...] = dot(cc, s_low)
    left = iota((Q, 128), 1) < 64
    for p in range(PAIRS):
        at = slice(p * 128, p * 128 + 128)
        a0 = lanes(a[:, 2 * p : 2 * p + 1])
        a1 = lanes(a[:, 2 * p + 1 : 2 * p + 2])
        w0 = jnp.exp2(a0 - b_t[2 * p : 2 * p + 1, :] + bias) * g
        w1 = jnp.exp2(a1 - b_t[2 * p + 1 : 2 * p + 2, :] + bias) * g
        w = jnp.concatenate([w0, w1], axis=1).astype(bf16)
        xp = act_out[:, at]
        zero = jnp.zeros_like(xp)
        xx = jnp.concatenate([jnp.where(left, xp, zero), jnp.where(left, zero, xp)], axis=0)
        y = dot(w, xx)
        ap = jnp.where(left, a0, a1)
        y += jnp.exp2(ap + carried) * cs[:, at]
        xf = xp.astype(f32)
        y_out[:, at] = y + dskip[0:1, at] * xf
        bp = jnp.where(left, lanes(b[:, 2 * p : 2 * p + 1]), lanes(b[:, 2 * p + 1 : 2 * p + 2]))
        a_end = ap[Q - 1 : Q, :]
        xe[:, at] = (jnp.exp2(a_end - bp + ending) * xf).astype(bf16)
        keep[0:1, at] = jnp.exp2(a_end + kept)
    b_turn = bb.astype(f32).T.astype(bf16)
    state[...] = state[...] * keep[0:1, :] + dot(b_turn, xe[...])


def full_spec(shape):
    return pl.BlockSpec(shape, lambda i, *_: (0,) * len(shape))


def scan_forward(ids, rows, conv_in, step_in, taps, head, dskip):
    return pl.pallas_call(
        fwd_kernel,
        grid_spec=pltpu.PrefetchScalarGridSpec(
            num_scalar_prefetch=1,
            grid=(CH,),
            in_specs=[
                pl.BlockSpec((Q, CONV), lambda i, *_: (i, 0)),
                pl.BlockSpec((Q, 128), lambda i, *_: (i, 0)),
                pl.BlockSpec((1, 8, Q), lambda i, *_: (i, 0, 0)),
                full_spec((8, CONV)),
                full_spec((8, 128)),
                full_spec((8, DI)),
            ],
            out_specs=[
                pl.BlockSpec((Q, DI), lambda i, *_: (i, 0)),
                pl.BlockSpec((Q, CONV), lambda i, *_: (i, 0)),
                pl.BlockSpec((Q, CONV), lambda i, *_: (i, 0)),
                pl.BlockSpec((1, N, DI), lambda i, *_: (i, 0, 0)),
            ],
            scratch_shapes=[
                pltpu.VMEM((N, DI), f32),
                pltpu.VMEM((Q + 8, CONV), f32),
                pltpu.VMEM((Q, DI), f32),
                pltpu.VMEM((Q, DI), bf16),
                pltpu.VMEM((8, DI), f32),
            ],
        ),
        out_shape=[
            jax.ShapeDtypeStruct((LEN, DI), f32),
            jax.ShapeDtypeStruct((LEN, CONV), bf16),
            jax.ShapeDtypeStruct((LEN, CONV), bf16),
            jax.ShapeDtypeStruct((CH, N, DI), bf16),
        ],
        name="scan_forward",
    )(ids, conv_in, step_in, rows, taps, head, dskip)


def bwd_kernel(ids_s, act, ds, cin, step, rows, taps, head, dskip, st, yg, y, gx_out, gconv, ghead, gskip, adj, cg, bz, xe, ye, keep, after, pick):
    i = pl.program_id(0)
    c = CH - 1 - i

    @pl.when(i == 0)
    def _():
        adj[...] = jnp.zeros_like(adj)
        cg[Q : Q + 8, :] = jnp.zeros((8, CONV), f32)
        after[...] = jnp.zeros_like(after)
        gconv[...] = jnp.zeros_like(gconv)
        ghead[...] = jnp.zeros_like(ghead)
        gskip[...] = jnp.zeros_like(gskip)
        pick[...] = jnp.where((iota((DI, 128), 0) >> 6) == iota((DI, 128), 1), 1.0, 0.0).astype(bf16)

    pre, dt, a, b = decay_terms(step[...], head)
    a_t = a.T
    bb = act[:, DI : DI + N]
    cc = act[:, DI + N :]
    g = dot_nt(bb, cc)
    turned = rows[0].T
    row_id = lanes(turned[:, 0:1])
    linked = (iota((Q, Q), 0) <= iota((Q, Q), 1)) & (row_id == rows[0, 0:1, :])
    bias = jnp.where(linked, 0.0, NEG)
    prev = jnp.where(c == 0, -1, ids_s[jnp.maximum(c * Q - 1, 0)])
    last = ids_s[c * Q + Q - 1]
    carried = jnp.where(row_id == prev.astype(f32), 0.0, NEG)
    ending = jnp.where(row_id == last.astype(f32), 0.0, NEG)
    kept = jnp.where(last == prev, 0.0, NEG)
    z_low = adj[...].astype(bf16)
    bz[...] = dot(bb, z_low)
    left = iota((Q, 128), 1) < 64
    g_grad = jnp.zeros((Q, Q), f32)
    dl = jnp.zeros((Q, 128), f32)
    own = jnp.zeros((Q, 128), f32)
    for p in range(PAIRS):
        at = slice(p * 128, p * 128 + 128)
        b0 = lanes(b[:, 2 * p : 2 * p + 1])
        b1 = lanes(b[:, 2 * p + 1 : 2 * p + 2])
        w0 = jnp.exp2(a_t[2 * p : 2 * p + 1, :] - b0 + bias)
        w1 = jnp.exp2(a_t[2 * p + 1 : 2 * p + 2, :] - b1 + bias)
        xp = act[:, at]
        yp = yg[:, at]
        zero = jnp.zeros_like(yp)
        yy = jnp.concatenate([jnp.where(left, yp, zero), jnp.where(left, zero, yp)], axis=0)
        m = dot_nt(xp, yy)
        g_grad += w0 * m[:, :Q] + w1 * m[:, Q:]
        w = jnp.concatenate([w0 * g, w1 * g], axis=1).astype(bf16)
        v = dot(w, yy)
        bp = jnp.where(left, b0, b1)
        ap = jnp.where(left, lanes(a[:, 2 * p : 2 * p + 1]), lanes(a[:, 2 * p + 1 : 2 * p + 2]))
        a_end = ap[Q - 1 : Q, :]
        fade = jnp.exp2(a_end - bp + ending)
        v += fade * bz[:, at]
        xf = xp.astype(f32)
        yf = yp.astype(f32)
        xg = v + dskip[0:1, at] * yf
        cg[0:Q, at] = xg
        r = yf * y[:, at] - xf * xg
        r_hi = r.astype(bf16)
        r_lo = (r - r_hi.astype(f32)).astype(bf16)
        e = pick[at, :]
        dl += dot(jnp.concatenate([r_hi, r_lo], axis=1), jnp.concatenate([e, e], axis=0))
        own += dot((xf * v).astype(bf16), e)
        xe[:, at] = (fade * xf).astype(bf16)
        ye[:, at] = (jnp.exp2(ap + carried) * yf).astype(bf16)
        keep[0:1, at] = jnp.exp2(a_end + kept)
        gskip[0:1, at] += jnp.sum(xf * yf, axis=0, keepdims=True)
    cg[0:Q, DI : DI + N] = dot(g_grad.astype(bf16), cc) + dot_nt(xe[...], z_low)
    cg[0:Q, DI + N :] = dot(g_grad.T.astype(bf16), bb) + dot_nt(ye[...], st[0])
    c_turn = cc.astype(f32).T.astype(bf16)
    adj_in = adj[...] * keep[0:1, :] + dot(c_turn, ye[...])
    adj[...] = adj_in

    upper = (iota((Q, Q), 0) <= iota((Q, Q), 1)).astype(f32)
    a_grad = jnp.dot(upper, dl, precision=highest, preferred_element_type=f32) + after[0:1, :]
    flux = jnp.sum(adj_in * st[0].astype(f32), axis=0, keepdims=True)
    flux_hi = flux.astype(bf16)
    flux_lo = (flux - flux_hi.astype(f32)).astype(bf16)
    both = dot(jnp.concatenate([flux_hi, flux_lo], axis=0), pick[...])
    after[0:1, :] = both[0:1, :] + both[1:2, :]
    rate = head[1:2, :]
    sig = 1.0 / (1.0 + jnp.exp(-pre))
    ratio = jnp.where(pre < -15.0, 1.0, sig / dt)
    step_grad = own * ratio + a_grad * rate * sig
    gx_out[:, CONV:] = step_grad[:, :H].astype(bf16)
    ghead[0:1, :] += jnp.sum(step_grad, axis=0, keepdims=True)
    ghead[1:2, :] += jnp.sum(a_grad * dt, axis=0, keepdims=True) * rate

    m1 = lanes(turned[:, 4:5])
    m2 = lanes(turned[:, 5:6])
    m3 = lanes(turned[:, 6:7])

    def conv_tile(j, _):
        at = pl.ds(pl.multiple_of(j * 128, 128), 128)
        s0 = cg[0:Q, at] * ds[:, at].astype(f32)
        cg[0:Q, at] = s0
        s1 = cg[1 : Q + 1, at] * m1
        s2 = cg[2 : Q + 2, at] * m2
        s3 = cg[3 : Q + 3, at] * m3
        gx = s0 * taps[3:4, at] + s1 * taps[2:3, at] + s2 * taps[1:2, at] + s3 * taps[0:1, at]
        gx_out[:, at] = gx.astype(bf16)
        xin = cin[:, at].astype(f32)
        gconv[3:4, at] += jnp.sum(s0 * xin, axis=0, keepdims=True)
        gconv[2:3, at] += jnp.sum(s1 * xin, axis=0, keepdims=True)
        gconv[1:2, at] += jnp.sum(s2 * xin, axis=0, keepdims=True)
        gconv[0:1, at] += jnp.sum(s3 * xin, axis=0, keepdims=True)
        gconv[4:5, at] += jnp.sum(s0, axis=0, keepdims=True)
        return 0

    lax.fori_loop(0, CONV // 128, conv_tile, 0)
    cg[Q : Q + 8, :] = cg[0:8, :]


def scan_backward(ids, rows, acts, dsilu, conv_in, step_in, taps, head, dskip, states, y_grad, y):
    rev = lambda i, *_: (CH - 1 - i, 0)
    rev3 = lambda i, *_: (CH - 1 - i, 0, 0)
    return pl.pallas_call(
        bwd_kernel,
        grid_spec=pltpu.PrefetchScalarGridSpec(
            num_scalar_prefetch=1,
            grid=(CH,),
            in_specs=[
                pl.BlockSpec((Q, CONV), rev),
                pl.BlockSpec((Q, CONV), rev),
                pl.BlockSpec((Q, CONV), rev),
                pl.BlockSpec((Q, 128), rev),
                pl.BlockSpec((1, 8, Q), rev3),
                full_spec((8, CONV)),
                full_spec((8, 128)),
                full_spec((8, DI)),
                pl.BlockSpec((1, N, DI), rev3),
                pl.BlockSpec((Q, DI), rev),
                pl.BlockSpec((Q, DI), rev),
            ],
            out_specs=[
                pl.BlockSpec((Q, WIDE), rev),
                full_spec((8, CONV)),
                full_spec((8, 128)),
                full_spec((8, DI)),
            ],
            scratch_shapes=[
                pltpu.VMEM((N, DI), f32),
                pltpu.VMEM((Q + 8, CONV), f32),
                pltpu.VMEM((Q, DI), f32),
                pltpu.VMEM((Q, DI), bf16),
                pltpu.VMEM((Q, DI), bf16),
                pltpu.VMEM((8, DI), f32),
                pltpu.VMEM((8, 128), f32),
                pltpu.VMEM((DI, 128), bf16),
            ],
        ),
        out_shape=[
            jax.ShapeDtypeStruct((LEN, WIDE), bf16),
            jax.ShapeDtypeStruct((8, CONV), f32),
            jax.ShapeDtypeStruct((8, 128), f32),
            jax.ShapeDtypeStruct((8, DI), f32),
        ],
        name="scan_backward",
    )(ids, acts, dsilu, conv_in, step_in, rows, taps, head, dskip, states, y_grad, y)


GB = 128


def gate_kernel(y, z, gn, gain, low_out, yg_out, zg_out, ggain):
    @pl.when(pl.program_id(0) == 0)
    def _():
        ggain[...] = jnp.zeros_like(ggain)

    zz = z[...].astype(f32)
    yy = y[...]
    sig = sigmoid(zz)
    silu = zz * sig
    gated = yy * silu
    r2 = lax.rsqrt(jnp.sum(gated * gated, axis=-1, keepdims=True) * (1.0 / DI) + norm_eps)
    unit = gated * r2
    k = gain[0:1, :]
    low_out[...] = (unit * k).astype(bf16)
    gnv = gn[...].astype(f32)
    ggain[0:1, :] += jnp.sum(gnv * unit, axis=0, keepdims=True)
    q = gnv * k
    coef = jnp.sum(q * unit, axis=-1, keepdims=True) * (1.0 / DI)
    gg = r2 * (q - unit * coef)
    yg_out[...] = (gg * silu).astype(bf16)
    zg_out[...] = (gg * yy * (sig + silu * (1.0 - sig))).astype(bf16)


def gate(y, z, gn, gain):
    blk = lambda: pl.BlockSpec((GB, DI), lambda i: (i, 0))
    return pl.pallas_call(
        gate_kernel,
        grid=(LEN // GB,),
        in_specs=[blk(), blk(), blk(), pl.BlockSpec((8, DI), lambda i: (0, 0))],
        out_specs=[blk(), blk(), blk(), pl.BlockSpec((8, DI), lambda i: (0, 0))],
        out_shape=[jax.ShapeDtypeStruct((LEN, DI), bf16)] * 3 + [jax.ShapeDtypeStruct((8, DI), f32)],
        name="gate",
    )(y, z, gn, gain)


beta_one = 0.9
beta_two = 0.95
learn_rate = 0.01
decay_rate = 0.1
adam_eps = 1e-08
adam_step = 3


def project_kernel(offs, lhs, *refs, count, half, tile, transposed, tail):
    parts = refs[: 2 * count - 1]
    outs = refs[2 * count - 1 : -3]
    weight, sems, back = refs[-3:]
    out, kept = outs[0], outs[-1]
    j = pl.program_id(0)

    @pl.when(j == 0)
    def _():
        copies = []
        for k, part in enumerate(parts):
            rows = pl.ds(pl.multiple_of(offs[k], half), part.shape[0])
            copies.append(pltpu.make_async_copy(part, weight.at[rows, :], sems.at[k]))
        for copy in copies:
            copy.start()
        for copy in copies:
            copy.wait()
        pltpu.make_async_copy(weight, kept, back.at[0]).start()
        if tail:
            outs[1][:, :tail] = dot(lhs[...], weight[:, weight.shape[1] - tail :])
            outs[1][:, tail:] = jnp.zeros((lhs.shape[0], 128 - tail), f32)

    at = pl.ds(pl.multiple_of(j * tile, tile), tile)
    if transposed:
        out[...] = dot_nt(lhs[...], weight[at, :]).astype(bf16)
    else:
        out[...] = dot(lhs[...], weight[:, at]).astype(bf16)

    @pl.when(j == pl.num_programs(0) - 1)
    def _():
        pltpu.make_async_copy(weight, kept, back.at[0]).wait()


def project(name, offs, lhs, parts, count, transposed=False, tail=0):
    own = parts[0].shape[0]
    rows, cols = own * count, parts[0].shape[1]
    wide = (rows if transposed else cols) - tail
    tile = 256
    outs = [jax.ShapeDtypeStruct((lhs.shape[0], wide), bf16)]
    specs = [pl.BlockSpec((lhs.shape[0], tile), lambda j, *_: (0, j))]
    if tail:
        outs.append(jax.ShapeDtypeStruct((lhs.shape[0], 128), f32))
        specs.append(pl.BlockSpec((lhs.shape[0], 128), lambda j, *_: (0, 0)))
    outs.append(jax.ShapeDtypeStruct((rows, cols), bf16))
    specs.append(pl.BlockSpec(memory_space=pl.ANY))

    def kernel(offs, lhs, *refs):
        project_kernel(offs, lhs, *refs, count=count, half=own // 2, tile=tile, transposed=transposed, tail=tail)

    return pl.pallas_call(
        kernel,
        grid_spec=pltpu.PrefetchScalarGridSpec(
            num_scalar_prefetch=1,
            grid=(wide // tile,),
            in_specs=[pl.BlockSpec(lhs.shape, lambda j, *_: (0, 0))]
            + [pl.BlockSpec(memory_space=pl.ANY)] * len(parts),
            out_specs=specs,
            scratch_shapes=[
                pltpu.VMEM((rows, cols), bf16),
                pltpu.SemaphoreType.DMA((len(parts),)),
                pltpu.SemaphoreType.DMA((1,)),
            ],
        ),
        out_shape=outs,
        name=name,
    )(offs, lhs, *parts)


def tree_sum(items):
    while len(items) > 1:
        items = [items[k] + items[k + 1] for k in range(0, len(items), 2)]
    return items[0]


def adam(weight, grad, first, second):
    first_new = beta_one * first + (1.0 - beta_one) * grad
    second_new = beta_two * second + (1.0 - beta_two) * grad * grad
    first_hat = first_new / (1.0 - beta_one**adam_step)
    second_hat = second_new / (1.0 - beta_two**adam_step)
    fresh = weight - learn_rate * (
        first_hat / (jnp.sqrt(second_hat) + adam_eps) + decay_rate * weight
    )
    return (fresh, first_new, second_new)


def pick_at(array, index, axis=0):
    return lax.dynamic_index_in_dim(array, index, axis, keepdims=False)


def make_body(replicas, owners):
    depth = replicas // 2

    def body(
        tokens,
        segment_ids,
        cotangent,
        lead_gain,
        inner_weight,
        conv_table,
        head_table,
        gate_gain,
        outer_weight,
        lead_first,
        inner_first,
        conv_first,
        head_first,
        gate_first,
        outer_first,
        lead_second,
        inner_second,
        conv_second,
        head_second,
        gate_second,
        outer_second,
    ):
        me = lax.axis_index("zero")
        rep = lax.axis_index("rep")
        core = rep & 1
        floor = rep >> 1

        def swap(value):
            return lax.ppermute(value, "rep", [(r, r ^ 1) for r in range(replicas)])

        def across(value, k):
            return lax.ppermute(value, "zero", [(i, i ^ k) for i in range(owners)])

        def up(value, k):
            return lax.ppermute(value, "rep", [(r, (((r >> 1) ^ k) << 1) | (r & 1)) for r in range(replicas)])

        def fetch(own):
            half = own.shape[0] // 2
            mine = lax.dynamic_slice_in_dim(own, core * half, half, 0)
            got = [across(mine, k) for k in range(1, owners)]
            return [own] + got + [swap(g) for g in got]

        def offsets(rows):
            half = rows // 2
            near = [(me ^ k) * rows + core * half for k in range(1, owners)]
            far = [(me ^ k) * rows + (1 - core) * half for k in range(1, owners)]
            return jnp.stack([me * rows] + near + far).astype(jnp.int32)

        def reduce_grad(send, keep):
            got = swap(send)
            parts = [
                (pick_at(keep, me ^ k).astype(f32) + pick_at(got, me ^ k).astype(f32)).astype(bf16)
                for k in range(owners)
            ]
            came = [across(parts[k], k) for k in range(1, owners)]
            total = tree_sum([v.astype(f32) for v in [parts[0]] + came]).astype(bf16)
            half, width = total.shape
            layers = total.reshape(depth, half // depth, width)
            parts = [pick_at(layers, floor ^ k) for k in range(depth)]
            came = [up(parts[k], k) for k in range(1, depth)]
            mine = tree_sum([v.astype(f32) for v in [parts[0]] + came]).astype(bf16)
            layers = lax.dynamic_update_index_in_dim(layers, mine, floor, 0)
            for k in range(1, depth):
                layers = lax.dynamic_update_index_in_dim(layers, up(mine, k), floor ^ k, 0)
            near = layers.reshape(half, width)
            far = swap(near)
            first = jnp.where(core == 0, near, far)
            second = jnp.where(core == 0, far, near)
            return jnp.concatenate([first, second], axis=0).astype(f32)

        def reduce_small(value):
            value = value.astype(bf16)
            value = (value.astype(f32) + swap(value).astype(f32)).astype(bf16)
            parts = [pick_at(value, me ^ k) for k in range(owners)]
            came = [across(parts[k], k) for k in range(1, owners)]
            total = tree_sum([v.astype(f32) for v in [parts[0]] + came]).astype(bf16)
            came = [up(total, k) for k in range(1, depth)]
            return tree_sum([v.astype(f32) for v in [total] + came])

        width_of = [v.size for v in (lead_gain, gate_gain, conv_table, head_table)]
        taken = sum(width_of)
        packed_rows = -(-taken // 2048) * 16

        def pack(values, lead_shape=()):
            flat = [v.reshape(lead_shape + (-1,)) for v in values]
            joined = jnp.concatenate(flat, axis=-1)
            fill = packed_rows * 128 - joined.shape[-1]
            joined = jnp.pad(joined, [(0, 0)] * len(lead_shape) + [(0, fill)])
            return joined.reshape(lead_shape + (packed_rows, 128))

        def unpack(value):
            flat = value.reshape(value.shape[:-2] + (-1,))
            at, out = 0, []
            for w in width_of:
                out.append(flat[..., at : at + w])
                at += w
            return out

        small = pack([v.astype(bf16) for v in (lead_gain, gate_gain, conv_table, head_table)])
        came = [small] + [across(small, k) for k in range(1, owners)]
        ordered = []
        for j in range(owners):
            value = came[0]
            for k in range(1, owners):
                value = jnp.where((me ^ k) == j, came[k], value)
            ordered.append(value)
        small_all = jnp.stack(ordered).astype(f32)
        lead_all, gate_all, conv_all, head_all = unpack(small_all)
        lead_low = lead_all.reshape(-1)
        gate_low = gate_all.reshape(-1)
        conv_low = conv_all.reshape(owners, K + 1, -1).transpose(1, 0, 2).reshape(K + 1, CONV)
        head_low = head_all.reshape(owners, 3, -1).transpose(1, 0, 2).reshape(3, H)

        mixed_shard = inner_weight[:, DI:].astype(bf16)
        gate_shard = inner_weight[:, :DI].astype(bf16)
        outer_shard = outer_weight.astype(bf16)
        in_parts = fetch(mixed_shard)
        out_parts = fetch(outer_shard)
        gate_parts = fetch(gate_shard)

        row_count, width = tokens.shape
        inner_rows = width // owners
        outer_rows = DI // owners
        ids = segment_ids
        rows = [ids.astype(f32)]
        for j in range(1, K):
            same = (ids[:-j] == ids[j:]).astype(f32)
            rows.append(jnp.concatenate([jnp.zeros((j,), f32), same]))
        for j in range(1, K):
            same = (ids[:-j] == ids[j:]).astype(f32)
            rows.append(jnp.concatenate([same, jnp.zeros((j,), f32)]))
        rows.append(jnp.zeros((LEN,), f32))
        rows = jnp.stack(rows).reshape(8, CH, Q).transpose(1, 0, 2)

        def rows8(value, cols):
            return jnp.pad(value, ((0, 8 - value.shape[0]), (0, cols - value.shape[1])))

        taps = rows8(conv_low, CONV)
        head = rows8(jnp.stack([head_low[0], -jnp.exp(head_low[1])]), 128)
        dskip = rows8(jnp.repeat(head_low[2], DI // H)[None], DI)
        gain = rows8(gate_low[None], DI)

        inputs = tokens.astype(f32)
        r1 = lax.rsqrt(jnp.mean(inputs * inputs, axis=-1, keepdims=True) + norm_eps)
        normed = (inputs * r1 * lead_low).astype(bf16)
        halves = normed.reshape(row_count, owners, 2, inner_rows // 2)
        turn_send = pick_at(halves, 1 - core, 2).reshape(row_count, -1).T
        turn_keep = pick_at(halves, core, 2).reshape(row_count, -1).T

        conv_in, step_in, in_full = project("project_in", offsets(inner_rows), normed, in_parts, owners, tail=H)
        y, acts, dsilu, states = scan_forward(ids, rows, conv_in, step_in, taps, head, dskip)
        gn_grad, outer_full = project("project_out_grad", offsets(outer_rows), cotangent, out_parts, owners, transposed=True)
        z, gate_full = project("project_gate", offsets(inner_rows), normed, gate_parts, owners)
        low, y_grad, z_grad, gate_sum = gate(y, z, gn_grad, gain)
        mixed = (inputs + dot(low, outer_full)).astype(bf16)

        low_halves = low.reshape(row_count, owners, 2, outer_rows // 2)

        def outer_part(which):
            part = pick_at(low_halves, which, 2)
            return jnp.einsum("tjr,te->jre", part, cotangent, preferred_element_type=f32).astype(bf16)

        outer_sum = reduce_grad(outer_part(1 - core), outer_part(core))

        def inner_part(turned, grad):
            return dot(turned, grad).astype(bf16).reshape(owners, inner_rows // 2, grad.shape[1])

        gate_in_sum = reduce_grad(inner_part(turn_send, z_grad), inner_part(turn_keep, z_grad))
        mix_grad, conv_sum, head_sum, skip_sum = scan_backward(
            ids, rows, acts, dsilu, conv_in, step_in, taps, head, dskip, states, y_grad, y
        )
        mix_in_sum = reduce_grad(inner_part(turn_send, mix_grad), inner_part(turn_keep, mix_grad))
        normed_grad = dot_nt(z_grad, gate_full) + dot_nt(mix_grad, in_full)
        q1 = normed_grad * lead_low
        back = r1 * (q1 - inputs * (r1 * r1 * jnp.mean(q1 * inputs, axis=-1, keepdims=True)))
        tokens_grad = (cotangent.astype(f32) + back).astype(bf16)
        lead_sum = jnp.sum(normed_grad * inputs * r1, axis=0)

        head_rows = jnp.concatenate([head_sum[:2, :H], skip_sum[0].reshape(1, H, DI // H).sum(-1)])

        def by_owner(value):
            return value.reshape(value.shape[0], owners, -1).transpose(1, 0, 2).reshape(owners, -1)

        small_sum = reduce_small(
            pack(
                [
                    lead_sum.reshape(owners, -1),
                    gate_sum[0].reshape(owners, -1),
                    by_owner(conv_sum[: K + 1]),
                    by_owner(head_rows),
                ],
                (owners,),
            )
        )
        lead_own, gate_own, conv_own, head_own = unpack(small_sum)
        conv_own = conv_own.reshape(conv_table.shape)
        head_own = head_own.reshape(head_table.shape)
        inner_own = jnp.concatenate([gate_in_sum, mix_in_sum], axis=1)

        sums = (lead_own, inner_own, conv_own, head_own, gate_own, outer_sum)
        weights = (lead_gain, inner_weight, conv_table, head_table, gate_gain, outer_weight)
        firsts = (lead_first, inner_first, conv_first, head_first, gate_first, outer_first)
        seconds = (lead_second, inner_second, conv_second, head_second, gate_second, outer_second)
        ups = [adam(*item) for item in zip(weights, sums, firsts, seconds)]
        return (
            (mixed, tokens_grad)
            + sums
            + tuple(up[0] for up in ups)
            + tuple(up[1] for up in ups)
            + tuple(up[2] for up in ups)
        )

    return body


def solution(mesh):
    flat, tall, wide = P("zero"), P("zero", None), P(None, "zero")
    group = (flat, tall, wide, wide, flat, tall)
    rows = P(("rep", "zero"), None)
    return jax.shard_map(
        make_body(mesh.shape["rep"], mesh.shape["zero"]),
        mesh=mesh,
        in_specs=(rows, P(("rep", "zero")), rows) + group * 3,
        out_specs=(rows, rows) + group * 4,
        check_vma=False,
    )
```

time: 822 us -> 613 us (0.75)
  matrix products: 268 us -> 56.3 us
  other arithmetic: 202 us -> 56.8 us
  Pallas kernels: 0 us -> 142 us
  blocking collectives: 72.3 us -> 0 us
  local copies, waits for them, and re-layouts: 78.9 us -> 147 us
  starting transfers between devices: 0.46 us -> 68.3 us
  waiting for transfers between devices: 167 us -> 130 us
  between operations: 22.6 us -> 2.14 us
    dot_general x50 -> x9, matrix products: 268 us -> 56.3 us  [the longest x5 31.2 us: dot(): return jnp.dot(a, b, preferred_element_type=f32)]
    pallas_call x0 -> x6, Pallas kernels: none -> 142 us  [the longest x1 54.7 us: scan_backward(): pl.pallas_call(bwd_kernel, grid_spec=pltpu.PrefetchScalarGridSpec(num_sca...]
    ppermute x0 -> x61, waiting for transfers between devices: none -> 130 us  [the longest x24 87.1 us: across(): return lax.ppermute(value, 'zero', [(i, i ^ k) for i in range(owners)])]
    ppermute x0 -> x61, starting transfers between devices: none -> 68.3 us  [the longest x21 34.3 us: up(): lax.ppermute(value, 'rep', [(r, (r >> 1 ^ k) << 1 | r & 1) for r in range...]
    reduce_sum x10 -> x2, other arithmetic: 60.9 us -> 0.59 us  [the longest x1 0.48 us: body(): r1 = lax.rsqrt(jnp.mean(inputs * inputs, axis=-1, keepdims=True) + norm_eps)]
    dynamic_slice x0 -> x9, local copies, waits for them, and re-layouts: none -> 50.4 us  [the longest x5 47.5 us: pick_at(): return lax.dynamic_index_in_dim(array, index, axis, keepdims=False)]
    psum x1 -> x0, waiting for transfers between devices: 50.1 us -> none  [body(): lax.psum(partial_sums[1].astype(jnp.bfloat16), 'rep').astype(jnp.float32)]
    reduce_scatter x2 -> x0, waiting for transfers between devices: 47.7 us -> none  [the longest x1 47.7 us: body(): lax.psum_scatter(inner_grad.astype(jnp.bfloat16), 'zero', scatter_dimensi...]
  transfers between devices with their start and end apart: 6 -> 61, of which waited for: 4 -> 21; matrix products, arithmetic and copies ran while one was open for 38% -> 31% of each run, Pallas kernels for 0% -> 4%
where the time goes in v1:
time: 613 us; the launch traced here: 602 us
  local copies, waits for them, and re-layouts  147 us (24%)
  Pallas kernels  142 us (23%)
  waiting for transfers between devices  130 us (21%)
  starting transfers between devices  68.3 us (11%)
  other arithmetic  56.8 us (9%)
  matrix products  56.3 us (9%)
    ppermute x24, waiting for transfers between devices, across(): return lax.ppermute(value, 'zero', [(i, i ^ k) for i in range(owners)])  87.1 us
    pallas_call x1, Pallas kernels, scan_backward(): pl.pallas_call(bwd_kernel, grid_spec=pltpu.PrefetchScalarGridSpec(num_sca...  54.7 us
    unnamed x105, local copies, waits for them, and re-layouts  51.5 us
    dynamic_slice x5, local copies, waits for them, and re-layouts, pick_at(): return lax.dynamic_index_in_dim(array, index, axis, keepdims=False)  47.5 us
    ppermute x21, waiting for transfers between devices, up(): lax.ppermute(value, 'rep', [(r, (r >> 1 ^ k) << 1 | r & 1) for r in range...  41.6 us
    pallas_call x3, Pallas kernels, project(): pl.pallas_call(kernel, grid_spec=pltpu.PrefetchScalarGridSpec(num_scalar_...  38 us
    ppermute x21, starting transfers between devices, up(): lax.ppermute(value, 'rep', [(r, (r >> 1 ^ k) << 1 | r & 1) for r in range...  34.3 us
    pallas_call x1, Pallas kernels, scan_forward(): pl.pallas_call(fwd_kernel, grid_spec=pltpu.PrefetchScalarGridSpec(num_sca...  33.5 us
  transfers between devices with their start and end apart: 61, of which 21 were waited for; matrix products, arithmetic and copies ran while one was open for 31% of the time, Pallas kernels for 4%

profile of v1, /device:TPU:0, one launch (start us, length us, event | category | flops | bytes accessed | tf_op | source)
XLA Modules:
  0.0 602.1 jit_solution(7785247793989387154)
XLA Ops:
  47.8 10.4 %collective-permute-done.11.refs_3_ = bf16[128,2048]{1,0:T(8,128)(2,1)S(1)} collective-permute-done((bf16[128,2048]{1,0:T(8,128)(2,1)}, bf16[128,2048]{1,0:T(8,128)(2,1)S(1)}, u32[]{:S(2)}, u32[]{:S(2)}) %collective-permute-start.11) | collective-permute-done | bytes 524320 | tf_op jit(solution)/shard_map/ppermute | solution.py:505
  60.6 20.6 %collective-permute-done.15.refs_1_ = bf16[256,1024]{1,0:T(8,128)(2,1)S(1)} collective-permute-done((bf16[256,1024]{1,0:T(8,128)(2,1)}, bf16[256,1024]{1,0:T(8,128)(2,1)S(1)}, u32[]{:S(2)}, u32[]{:S(2)}) %collective-permute-start.15) | collective-permute-done | bytes 524320 | tf_op jit(solution)/shard_map/ppermute | solution.py:505
  82.9 20.9 %collective-permute-done.17.refs_3_ = bf16[256,1024]{1,0:T(8,128)(2,1)} collective-permute-done((bf16[256,1024]{1,0:T(8,128)(2,1)}, bf16[256,1024]{1,0:T(8,128)(2,1)}, u32[]{:S(2)}, u32[]{:S(2)}) %collective-permute-start.17) | collective-permute-done | bytes 524320 | tf_op jit(solution)/shard_map/ppermute | solution.py:505
  112.0 8.5 %constant_dynamic-slice_fusion.6 = (bf16[1024,4,1,128]{3,2,1,0:T(2,128)(2,1)}, bf16[1024,4,1,128]{3,2,1,0:T(2,128)(2,1)}) fusion(bf16[1024,4,2,128]{3,2,1,0:T(2,128)(2,1)} %reshape.287, s32[]{:T(128)S(6)} %select_n.237, s32[]{:T(128)S(6)} %select_n.236), kind=kLoop, calls=%fused_computation.135 | loop fusion | bytes 4194312 | tf_op jit(solution)/shard_map/jit(dynamic_index_in_dim)/dynamic_slice | solution.py:467
  136.5 12.2 %project_gate.1 = (bf16[1024,2048]{1,0:T(8,128)(2,1)}, bf16[1024,2048]{1,0:T(8,128)(2,1)}) custom-call(s32[7]{0:T(128)} %stack.106.offs, bf16[1024,1024]{1,0:T(8,128)(2,1)} %copy-done, bf16[256,2048]{1,0:T(8,128)(2,1)} %copy-done.10, bf16[128,2048]{1,0:T(8,128)(2,1)} %collective-permute-done.9.refs_1_, bf16[128,2048]{1,0:T(8,128)(2,1)} %collective-permute-done.10.refs_2_, ...), custom_call_target="tpu_custom_call" | custom-call | tf_op jit(solution)/shard_map/project_gate/pallas_call | solution.py:430
  148.8 12.2 %project_out_grad.1 = (bf16[1024,2048]{1,0:T(8,128)(2,1)}, bf16[2048,1024]{1,0:T(8,128)(2,1)}) custom-call(s32[7]{0:T(128)} %stack.128.offs, bf16[1024,1024]{1,0:T(8,128)(2,1)} %lhs.14, bf16[512,1024]{1,0:T(8,128)(2,1)} %copy-done.9, bf16[256,1024]{1,0:T(8,128)(2,1)} %copy-done.25, bf16[256,1024]{1,0:T(8,128)(2,1)} %collective-permute-done.16.refs_2_, ...), custom_call_target="tpu_custom_call" | custom-call | tf_op jit(solution)/shard_map/project_out_grad/pallas_call | solution.py:430
  167.4 13.6 %project_in.1 = (bf16[1024,2304]{1,0:T(8,128)(2,1)}, f32[1024,128]{1,0:T(8,128)}, bf16[1024,2336]{1,0:T(8,128)(2,1)}) custom-call(s32[7]{0:T(128)} %stack.106.offs, bf16[1024,1024]{1,0:T(8,128)(2,1)} %copy-done, bf16[256,2336]{1,0:T(8,128)(2,1)} %copy-done.8, bf16[128,2336]{1,0:T(8,128)(2,1)} %copy.95.refs_1_, bf16[128,2336]{1,0:T(8,128)(2,1)} %copy.96.refs_2_, ...), custom_call_target="tpu_custom_call" | custom-call | tf_op jit(solution)/shard_map/project_in/pallas_call | solution.py:430
  181.1 33.5 %scan_forward.1 = (f32[1024,2048]{1,0:T(8,128)}, bf16[1024,2304]{1,0:T(8,128)(2,1)}, bf16[1024,2304]{1,0:T(8,128)(2,1)}, bf16[8,128,2048]{2,1,0:T(8,128)(2,1)}) custom-call(s32[1024]{0:T(1024)} %ids_s.3, bf16[1024,2304]{1,0:T(8,128)(2,1)} %get-tuple-element.45.cin, f32[1024,128]{1,0:T(8,128)} %get-tuple-element.46.step, f32[8,8,128]{2,1,0:T(8,128)} %bitcast.246, ...), custom_call_target="tpu_custom_call" | custom-call | tf_op jit(solution)/shard_map/scan_forward/pallas_call | solution.py:137
  214.5 15.7 %gate.1 = (bf16[1024,2048]{1,0:T(8,128)(2,1)}, bf16[1024,2048]{1,0:T(8,128)(2,1)}, bf16[1024,2048]{1,0:T(8,128)(2,1)}, f32[8,2048]{1,0:T(8,128)}) custom-call(f32[1024,2048]{1,0:T(8,128)} %get-tuple-element.47.y, bf16[1024,2048]{1,0:T(8,128)(2,1)} %get-tuple-element.48.z, bf16[1024,2048]{1,0:T(8,128)(2,1)} %get-tuple-element.49.gn, f32[8,2048]{1,0:T(8,128)} %pad.32.gain), custom_call_target="tpu_custom_call" | custom-call | tf_op jit(solution)/shard_map/gate/pallas_call | solution.py:363
  239.9 54.7 %scan_backward.1 = (bf16[1024,2336]{1,0:T(8,128)(2,1)}, f32[8,2304]{1,0:T(8,128)}, f32[8,128]{1,0:T(8,128)}, f32[8,2048]{1,0:T(8,128)}) custom-call(s32[1024]{0:T(1024)} %ids_s.3, bf16[1024,2304]{1,0:T(8,128)(2,1)} %get-tuple-element.54.act, bf16[1024,2304]{1,0:T(8,128)(2,1)} %get-tuple-element.55.ds, bf16[1024,2304]{1,0:T(8,128)(2,1)} %get-tuple-element.45.cin, ...), custom_call_target="tpu_custom_call" | custom-call | tf_op jit(solution)/shard_map/scan_backward/pallas_call | solution.py:290
  294.6 7.7 %convolution_convert_fusion.1 = bf16[512,2336]{0,1:T(8,128)(2,1)} fusion(bf16[1024,512]{0,1:T(8,128)(2,1)S(1)} %bitcast.244, bf16[1024,2336]{1,0:T(8,128)(2,1)} %get-tuple-element.58), kind=kOutput, calls=%fused_computation.11 | convolution fusion | flops 2450669568 | bytes 8224768 | tf_op jit(solution)/shard_map/dot_general | solution.py:31
  309.1 7.8 %reshape.300 = bf16[1024,4,2,256]{3,2,1,0:T(2,128)(2,1)} reshape(bf16[1024,2048]{1,0:T(8,128)(2,1)} %get-tuple-element.50) | data formatting | bytes 8388608 | tf_op jit(solution)/shard_map/reshape | solution.py:630
  316.9 11.3 %constant_dynamic-slice_fusion.1 = (bf16[1024,4,1,256]{3,2,1,0:T(2,128)(2,1)}, bf16[1024,4,1,256]{3,2,1,0:T(2,128)(2,1)}) fusion(bf16[1024,4,2,256]{3,2,1,0:T(2,128)(2,1)} %reshape.300, s32[]{:T(128)S(6)} %select_n.236, s32[]{:T(128)S(6)} %select_n.237), kind=kLoop, calls=%fused_computation.130 | loop fusion | bytes 8388616 | tf_op jit(solution)/shard_map/jit(dynamic_index_in_dim)/dynamic_slice | solution.py:467
  328.2 10.8 %copy.116 = bf16[1024,4,1,256]{0,3,1,2:T(8,128)(2,1)} copy(bf16[1024,4,1,256]{3,2,1,0:T(2,128)(2,1)} %get-tuple-element.147) | data formatting | bytes 4194304 | tf_op jit(solution)/shard_map/jit(dynamic_index_in_dim)/dynamic_slice | solution.py:467
  344.3 10.5 %copy.115 = bf16[1024,4,1,256]{0,3,1,2:T(8,128)(2,1)} copy(bf16[1024,4,1,256]{3,2,1,0:T(2,128)(2,1)} %get-tuple-element.146) | data formatting | bytes 4194304 | tf_op jit(solution)/shard_map/jit(dynamic_index_in_dim)/dynamic_slice | solution.py:467
  356.1 9.2 %fusion.78 = f32[1024,1024]{1,0:T(8,128)S(1)} fusion(bf16[1024,2336]{1,0:T(8,128)(2,1)} %get-tuple-element.58, bf16[1024,2336]{1,0:T(8,128)(2,1)} %get-tuple-element.59), kind=kOutput, calls=%fused_computation.194 | convolution fusion | flops 4898947072 | bytes 13762560 | tf_op jit(solution)/shard_map/dot_general | solution.py:35
  365.4 7.1 %fusion.11 = (bf16[1024]{0:T(1024)(128)(2,1)S(1)}, f32[1024]{0:T(1024)S(1)}, f32[1024,1024]{1,0:T(8,128)}) fusion(bf16[1024,1024]{1,0:T(8,128)(2,1)S(1)} %copy-done.2, f32[1024]{0:T(1024)S(1)} %add_rsqrt_fusion, f32[1024]{0:T(1024)S(1)} %bitcast.251, f32[1024,1024]{1,0:T(8,128)S(1)} %fusion.78, bf16[1024,2048]{1,0:T(8,128)(2,1)S(1)} %copy-done.45, ...), kind=kOutput, calls=%fused_computation.22 | convolution fusion | flops 4303353856 | bytes 18888704 | tf_op jit(solution)/shard_map/dot_general | solution.py:35
  374.2 9.4 %fusion.4 = bf16[1024,1024]{1,0:T(8,128)(2,1)} fusion(bf16[1024,1024]{1,0:T(8,128)(2,1)S(1)} %copy-done.2, bf16[1024,2048]{1,0:T(8,128)(2,1)} %get-tuple-element.50, bf16[2048,1024]{1,0:T(8,128)(2,1)} %get-tuple-element.51), kind=kOutput, calls=%fused_computation.15 | convolution fusion | flops 4298113024 | bytes 12582912 | tf_op jit(solution)/shard_map/dot_general | solution.py:31
  433.4 10.4 %collective-permute-done.30 = bf16[128,2048]{1,0:T(8,128)(2,1)S(1)} collective-permute-done((bf16[128,2048]{1,0:T(8,128)(2,1)S(1)}, bf16[128,2048]{1,0:T(8,128)(2,1)S(1)}, u32[]{:S(2)}, u32[]{:S(2)}) %collective-permute-start.30) | collective-permute-done | bytes 524320 | tf_op jit(solution)/shard_map/ppermute | solution.py:505
  454.3 12.0 %collective-permute-done.52 = bf16[256,1024]{1,0:T(8,128)(2,1)S(1)} collective-permute-done((bf16[256,1024]{1,0:T(8,128)(2,1)S(1)}, bf16[256,1024]{1,0:T(8,128)(2,1)S(1)}, u32[]{:S(2)}, u32[]{:S(2)}) %collective-permute-start.52) | collective-permute-done | bytes 524320 | tf_op jit(solution)/shard_map/ppermute | solution.py:505
  482.1 8.4 %collective-permute-done.55 = bf16[64,1024]{1,0:T(8,128)(2,1)S(1)} collective-permute-done((bf16[64,1024]{1,0:T(8,128)(2,1)S(1)}, bf16[64,1024]{1,0:T(8,128)(2,1)S(1)}, u32[]{:S(2)}, u32[]{:S(2)}) %collective-permute-start.55) | collective-permute-done | bytes 131104 | tf_op jit(solution)/shard_map/ppermute | solution.py:508
  523.1 6.8 %collective-permute-done.44 = bf16[32,2336]{1,0:T(8,128)(2,1)S(1)} collective-permute-done((bf16[32,2336]{1,0:T(8,128)(2,1)S(1)}, bf16[32,2336]{1,0:T(8,128)(2,1)S(1)}, u32[]{:S(2)}, u32[]{:S(2)}) %collective-permute-start.44) | collective-permute-done | bytes 149536 | tf_op jit(solution)/shard_map/ppermute | solution.py:508
  539.0 8.7 %collective-permute-done.47 = bf16[32,2336]{1,0:T(8,128)(2,1)S(1)} collective-permute-done((bf16[32,2336]{1,0:T(8,128)(2,1)S(1)}, bf16[32,2336]{1,0:T(8,128)(2,1)S(1)}, u32[]{:S(2)}, u32[]{:S(2)}) %collective-permute-start.47) | collective-permute-done | bytes 149536 | tf_op jit(solution)/shard_map/ppermute | solution.py:508
  561.3 16.8 %multiply_subtract_fusion = (f32[256,4384]{1,0:T(8,128)}, f32[256,4384]{1,0:T(8,128)}, f32[256,4384]{1,0:T(8,128)}) fusion(f32[256,4384]{1,0:T(8,128)} %copy.91, bf16[128,2336]{1,0:T(8,128)(2,1)S(1)} %get-tuple-element.161, bf16[128,2336]{1,0:T(8,128)(2,1)S(1)} %get-tuple-element.160, bf16[128,2048]{1,0:T(8,128)(2,1)S(1)} %copy-done.15, ...), kind=kLoop, calls=%fused_computation.8 | loop fusion | flops 25812992 | bytes 29179904 | tf_op jit(solution)/shard_map/sub | solution.py:460
  (348 shorter events, 260.9 us)
Async XLA Ops:
  3.7 38.5 %collective-permute-start = (bf16[32,128]{1,0:T(8,128)(2,1)S(1)}, bf16[32,128]{1,0:T(8,128)(2,1)S(1)}, u32[]{:S(2)}, u32[]{:S(2)}) collective-permute-start(bf16[32,128]{1,0:T(8,128)(2,1)S(1)} %pad_bitcast_fusion.1), channel_id=1, source_target_pairs={{0,3},{1,2},{2,1},{3,0},{4,7},{5,6},{6,5},{7,4},{8,11},{9,10},{10,... | collective-permute-start | bytes 24584 | tf_op jit(solution)/shard_map/ppermute | solution.py:505
  7.6 34.8 %collective-permute-start.1 = (bf16[32,128]{1,0:T(8,128)(2,1)S(1)}, bf16[32,128]{1,0:T(8,128)(2,1)S(1)}, u32[]{:S(2)}, u32[]{:S(2)}) collective-permute-start(bf16[32,128]{1,0:T(8,128)(2,1)S(1)} %pad_bitcast_fusion.1), channel_id=1, source_target_pairs={{0,2},{1,3},{2,0},{3,1},{4,6},{5,7},{6,4},{7,5},{8,10},{9,11},{10,... | collective-permute-start | bytes 24584 | tf_op jit(solution)/shard_map/ppermute | solution.py:505
  8.2 37.0 %collective-permute-start.2 = (bf16[32,128]{1,0:T(8,128)(2,1)S(1)}, bf16[32,128]{1,0:T(8,128)(2,1)S(1)}, u32[]{:S(2)}, u32[]{:S(2)}) collective-permute-start(bf16[32,128]{1,0:T(8,128)(2,1)S(1)} %pad_bitcast_fusion.1), channel_id=1, source_target_pairs={{0,1},{1,0},{2,3},{3,2},{4,5},{5,4},{6,7},{7,6},{8,9},{9,8},{10,11... | collective-permute-start | bytes 24584 | tf_op jit(solution)/shard_map/ppermute | solution.py:505
  42.4 61.4 %collective-permute-start.5 = (bf16[128,2336]{0,1:T(8,128)(2,1)S(1)}, bf16[128,2336]{0,1:T(8,128)(2,1)}, u32[]{:S(2)}, u32[]{:S(2)}) collective-permute-start(bf16[128,2336]{0,1:T(8,128)(2,1)S(1)} %copy-done.23), channel_id=1, source_target_pairs={{0,3},{1,2},{2,1},{3,0},{4,7},{5,6},{6,5},{7,4},{8,11},{9,10},{10,... | collective-permute-start | bytes 1794056 | tf_op jit(solution)/shard_map/ppermute | solution.py:505
  45.1 36.1 %collective-permute-start.15 = (bf16[256,1024]{1,0:T(8,128)(2,1)}, bf16[256,1024]{1,0:T(8,128)(2,1)S(1)}, u32[]{:S(2)}, u32[]{:S(2)}) collective-permute-start(bf16[256,1024]{1,0:T(8,128)(2,1)} %constant_dynamic-slice_fusion.12), channel_id=1, source_target_pairs={{0,1},{1,0},{2,3},{3,2},{4,5},{5,4},{6,7},{7,6},{8,9},{9,8},{10,11... | collective-permute-start | bytes 1572872 | tf_op jit(solution)/shard_map/ppermute | solution.py:505
  45.8 58.7 %collective-permute-start.3 = (bf16[128,2336]{0,1:T(8,128)(2,1)S(1)}, bf16[128,2336]{0,1:T(8,128)(2,1)}, u32[]{:S(2)}, u32[]{:S(2)}) collective-permute-start(bf16[128,2336]{0,1:T(8,128)(2,1)S(1)} %copy-done.23), channel_id=1, source_target_pairs={{0,1},{1,0},{2,3},{3,2},{4,5},{5,4},{6,7},{7,6},{8,9},{9,8},{10,11... | collective-permute-start | bytes 1794056 | tf_op jit(solution)/shard_map/ppermute | solution.py:505
  47.3 35.6 %collective-permute-start.16 = (bf16[256,1024]{1,0:T(8,128)(2,1)}, bf16[256,1024]{1,0:T(8,128)(2,1)}, u32[]{:S(2)}, u32[]{:S(2)}) collective-permute-start(bf16[256,1024]{1,0:T(8,128)(2,1)} %constant_dynamic-slice_fusion.12), channel_id=1, source_target_pairs={{0,2},{1,3},{2,0},{3,1},{4,6},{5,7},{6,4},{7,5},{8,10},{9,11},{10,... | collective-permute-start | bytes 1572872 | tf_op jit(solution)/shard_map/ppermute | solution.py:505
  58.2 45.6 %collective-permute-start.17 = (bf16[256,1024]{1,0:T(8,128)(2,1)}, bf16[256,1024]{1,0:T(8,128)(2,1)}, u32[]{:S(2)}, u32[]{:S(2)}) collective-permute-start(bf16[256,1024]{1,0:T(8,128)(2,1)} %constant_dynamic-slice_fusion.12), channel_id=1, source_target_pairs={{0,3},{1,2},{2,1},{3,0},{4,7},{5,6},{6,5},{7,4},{8,11},{9,10},{10,... | collective-permute-start | bytes 1572872 | tf_op jit(solution)/shard_map/ppermute | solution.py:505
  104.6 56.3 %collective-permute-start.8 = (bf16[128,2336]{0,1:T(8,128)(2,1)}, bf16[128,2336]{0,1:T(8,128)(2,1)}, u32[]{:S(2)}, u32[]{:S(2)}) collective-permute-start(bf16[128,2336]{0,1:T(8,128)(2,1)} %collective-permute-done.5), channel_id=1, source_target_pairs={{0,4},{4,0},{8,12},{12,8},{16,20},{20,16},{24,28},{28,24},{1,5},{5... | collective-permute-start | bytes 1794056 | tf_op jit(solution)/shard_map/ppermute | solution.py:502
  105.1 58.0 %collective-permute-start.6 = (bf16[128,2336]{0,1:T(8,128)(2,1)}, bf16[128,2336]{0,1:T(8,128)(2,1)}, u32[]{:S(2)}, u32[]{:S(2)}) collective-permute-start(bf16[128,2336]{0,1:T(8,128)(2,1)} %collective-permute-done.3), channel_id=1, source_target_pairs={{0,4},{4,0},{8,12},{12,8},{16,20},{20,16},{24,28},{28,24},{1,5},{5... | collective-permute-start | bytes 1794056 | tf_op jit(solution)/shard_map/ppermute | solution.py:502
  106.1 59.2 %collective-permute-start.7 = (bf16[128,2336]{0,1:T(8,128)(2,1)}, bf16[128,2336]{0,1:T(8,128)(2,1)}, u32[]{:S(2)}, u32[]{:S(2)}) collective-permute-start(bf16[128,2336]{0,1:T(8,128)(2,1)} %collective-permute-done.4), channel_id=1, source_target_pairs={{0,4},{4,0},{8,12},{12,8},{16,20},{20,16},{24,28},{28,24},{1,5},{5... | collective-permute-start | bytes 1794056 | tf_op jit(solution)/shard_map/ppermute | solution.py:502
  111.5 37.3 %collective-permute-start.19 = (bf16[256,1024]{1,0:T(8,128)(2,1)}, bf16[256,1024]{1,0:T(8,128)(2,1)}, u32[]{:S(2)}, u32[]{:S(2)}) collective-permute-start(bf16[256,1024]{1,0:T(8,128)(2,1)} %collective-permute-done.16.refs_2_), channel_id=1, source_target_pairs={{0,4},{4,0},{8,12},{12,8},{16,20},{20,16},{24,28},{28,24},{1,5},{5... | collective-permute-start | bytes 1572872 | tf_op jit(solution)/shard_map/ppermute | solution.py:502
  111.8 36.9 %collective-permute-start.20 = (bf16[256,1024]{1,0:T(8,128)(2,1)}, bf16[256,1024]{1,0:T(8,128)(2,1)}, u32[]{:S(2)}, u32[]{:S(2)}) collective-permute-start(bf16[256,1024]{1,0:T(8,128)(2,1)} %collective-permute-done.17.refs_3_), channel_id=1, source_target_pairs={{0,4},{4,0},{8,12},{12,8},{16,20},{20,16},{24,28},{28,24},{1,5},{5... | collective-permute-start | bytes 1572872 | tf_op jit(solution)/shard_map/ppermute | solution.py:502
  306.7 107.0 %collective-permute-start.28 = (bf16[4,128,2048]{2,1,0:T(8,128)(2,1)}, bf16[4,128,2048]{2,1,0:T(8,128)(2,1)}, u32[]{:S(2)}, u32[]{:S(2)}) collective-permute-start(bf16[4,128,2048]{2,1,0:T(8,128)(2,1)} %bitcast.35), channel_id=1, source_target_pairs={{0,4},{4,0},{8,12},{12,8},{16,20},{20,16},{24,28},{28,24},{1,5},{5... | collective-permute-start | bytes 6291464 | tf_op jit(solution)/shard_map/ppermute | solution.py:502
  309.0 114.4 %collective-permute-start.39 = (bf16[4,128,2336]{1,2,0:T(8,128)(2,1)}, bf16[4,128,2336]{1,2,0:T(8,128)(2,1)}, u32[]{:S(2)}, u32[]{:S(2)}) collective-permute-start(bf16[4,128,2336]{1,2,0:T(8,128)(2,1)} %bitcast.228), channel_id=1, source_target_pairs={{0,4},{4,0},{8,12},{12,8},{16,20},{20,16},{24,28},{28,24},{1,5},{5... | collective-permute-start | bytes 7176200 | tf_op jit(solution)/shard_map/ppermute | solution.py:502
  391.0 28.8 %collective-permute-start.50 = (bf16[4,256,1024]{2,1,0:T(8,128)(2,1)}, bf16[4,256,1024]{2,1,0:T(8,128)(2,1)}, u32[]{:S(2)}, u32[]{:S(2)}) collective-permute-start(bf16[4,256,1024]{2,1,0:T(8,128)(2,1)} %fusion.24), channel_id=1, source_target_pairs={{0,4},{4,0},{8,12},{12,8},{16,20},{20,16},{24,28},{28,24},{1,5},{5... | collective-permute-start | bytes 6291464 | tf_op jit(solution)/shard_map/ppermute | solution.py:502
  421.9 31.8 %collective-permute-start.51 = (bf16[256,1024]{1,0:T(8,128)(2,1)S(1)}, bf16[256,1024]{1,0:T(8,128)(2,1)S(1)}, u32[]{:S(2)}, u32[]{:S(2)}) collective-permute-start(bf16[256,1024]{1,0:T(8,128)(2,1)S(1)} %get-tuple-element.143), channel_id=1, source_target_pairs={{0,1},{1,0},{2,3},{3,2},{4,5},{5,4},{6,7},{7,6},{8,9},{9,8},{10,11... | collective-permute-start | bytes 1572872 | tf_op jit(solution)/shard_map/ppermute | solution.py:505
  423.4 42.9 %collective-permute-start.52 = (bf16[256,1024]{1,0:T(8,128)(2,1)S(1)}, bf16[256,1024]{1,0:T(8,128)(2,1)S(1)}, u32[]{:S(2)}, u32[]{:S(2)}) collective-permute-start(bf16[256,1024]{1,0:T(8,128)(2,1)S(1)} %get-tuple-element.145), channel_id=1, source_target_pairs={{0,2},{1,3},{2,0},{3,1},{4,6},{5,7},{6,4},{7,5},{8,10},{9,11},{10,... | collective-permute-start | bytes 1572872 | tf_op jit(solution)/shard_map/ppermute | solution.py:505
  431.1 36.8 %collective-permute-start.53 = (bf16[256,1024]{1,0:T(8,128)(2,1)S(1)}, bf16[256,1024]{1,0:T(8,128)(2,1)S(1)}, u32[]{:S(2)}, u32[]{:S(2)}) collective-permute-start(bf16[256,1024]{1,0:T(8,128)(2,1)S(1)} %get-tuple-element.144), channel_id=1, source_target_pairs={{0,3},{1,2},{2,1},{3,0},{4,7},{5,6},{6,5},{7,4},{8,11},{9,10},{10,... | collective-permute-start | bytes 1572872 | tf_op jit(solution)/shard_map/ppermute | solution.py:505
  443.8 69.7 %collective-permute-start.40 = (bf16[128,2336]{0,1:T(8,128)(2,1)S(1)}, bf16[128,2336]{0,1:T(8,128)(2,1)S(1)}, u32[]{:S(2)}, u32[]{:S(2)}) collective-permute-start(bf16[128,2336]{0,1:T(8,128)(2,1)S(1)} %get-tuple-element.155), channel_id=1, source_target_pairs={{0,1},{1,0},{2,3},{3,2},{4,5},{5,4},{6,7},{7,6},{8,9},{9,8},{10,11... | collective-permute-start | bytes 1794056 | tf_op jit(solution)/shard_map/ppermute | solution.py:505
  444.1 69.4 %collective-permute-start.41 = (bf16[128,2336]{0,1:T(8,128)(2,1)S(1)}, bf16[128,2336]{0,1:T(8,128)(2,1)S(1)}, u32[]{:S(2)}, u32[]{:S(2)}) collective-permute-start(bf16[128,2336]{0,1:T(8,128)(2,1)S(1)} %get-tuple-element.157), channel_id=1, source_target_pairs={{0,2},{1,3},{2,0},{3,1},{4,6},{5,7},{6,4},{7,5},{8,10},{9,11},{10,... | collective-permute-start | bytes 1794056 | tf_op jit(solution)/shard_map/ppermute | solution.py:505
  480.6 32.9 %collective-permute-start.42 = (bf16[128,2336]{0,1:T(8,128)(2,1)S(1)}, bf16[128,2336]{0,1:T(8,128)(2,1)S(1)}, u32[]{:S(2)}, u32[]{:S(2)}) collective-permute-start(bf16[128,2336]{0,1:T(8,128)(2,1)S(1)} %get-tuple-element.156), channel_id=1, source_target_pairs={{0,3},{1,2},{2,1},{3,0},{4,7},{5,6},{6,5},{7,4},{8,11},{9,10},{10,... | collective-permute-start | bytes 1794056 | tf_op jit(solution)/shard_map/ppermute | solution.py:505
  512.8 36.0 %collective-permute-start.38 = (bf16[128,2048]{1,0:T(8,128)(2,1)S(1)}, bf16[128,2048]{1,0:T(8,128)(2,1)}, u32[]{:S(2)}, u32[]{:S(2)}) collective-permute-start(bf16[128,2048]{1,0:T(8,128)(2,1)S(1)} %bitcast.238), channel_id=1, source_target_pairs={{0,4},{4,0},{8,12},{12,8},{16,20},{20,16},{24,28},{28,24},{1,5},{5... | collective-permute-start | bytes 1572872 | tf_op jit(solution)/shard_map/ppermute | solution.py:502
  520.4 30.6 %collective-permute-start.60 = (bf16[256,1024]{1,0:T(8,128)(2,1)}, bf16[256,1024]{1,0:T(8,128)(2,1)}, u32[]{:S(2)}, u32[]{:S(2)}) collective-permute-start(bf16[256,1024]{1,0:T(8,128)(2,1)} %bitcast.82), channel_id=1, source_target_pairs={{0,4},{4,0},{8,12},{12,8},{16,20},{20,16},{24,28},{28,24},{1,5},{5... | collective-permute-start | bytes 1572872 | tf_op jit(solution)/shard_map/ppermute | solution.py:502
  (83 other events, 1045.7 us)
